TPU v7x, 32 devices: a whole 2x2x4 slice. The times are simulated.
32 devices in a mesh: ctx: 8 (over y, x, core), head: 4 (over z).
Axes of the slice: x: 2, y: 2, z: 4, core: 2. Of those that a mesh axis runs over, the one named last changes fastest.
Arguments:
- tokens_x: bfloat16 [4096, 8192], P('ctx', 'head'), may hold values from -121 to 121
- raw_dt: float32 [128, 4096], P('head', 'ctx'), may hold values from -4 to 4
- in_b: bfloat16 [4096, 128], P('ctx'), may hold values from -0.5 to 0.5
- in_c: bfloat16 [4096, 128], P('ctx'), may hold values from -0.5 to 0.5
- decay_rate: float32 [128], P('head'), may hold values from 4.8828125e-06 to 2
- skip_gain: float32 [128], P('head'), may hold values from 0.5 to 1.5
- step_bias: float32 [128], P('head'), may hold values from -5 to -3
- grad_y: bfloat16 [4096, 8192], P('ctx', 'head'), may hold values from -121 to 121
Outputs:
- grad_x: bfloat16 [4096, 8192], P('ctx', 'head')
- grad_raw_dt: float32 [128, 4096], P('head', 'ctx')
- grad_b: float32 [4096, 128], P('ctx')
- grad_c: float32 [4096, 128], P('ctx')
- grad_rate: float32 [128], P('head')
- grad_skip: float32 [128], P('head')
- grad_bias: float32 [128], P('head')
All inputs are finite; a program needn't handle non-finite values.
Results may differ from a plain program's by a relative error of at most 0.001.
Values sent between devices are 32-bit elements; how exact they have to be, the bound alone decides.
A program may use at most 128 MiB of HBM per device.

v0:
```python
import jax
import jax.numpy as jnp
from jax import lax
from jax.experimental import pallas as pl
from jax.experimental.pallas import tpu as pltpu
from jax.sharding import PartitionSpec as P

CHUNK = 128
GROUP = 8
F32 = jnp.float32
BF16 = jnp.bfloat16
HIGH = lax.Precision.HIGHEST
NT = (((1,), (1,)), ((), ()))
PARAMS = pltpu.CompilerParams(vmem_limit_bytes=56 << 20)


def mm(a, b):
    return jnp.dot(a, b, preferred_element_type=F32)


def mm_nt(a, b):
    return lax.dot_general(a, b, NT, preferred_element_type=F32)


def split(a):
    high = a.astype(BF16)
    return high, (a - high.astype(F32)).astype(BF16)


def softplus(v):
    return jnp.maximum(v, 0.0) + jnp.log1p(jnp.exp(-jnp.abs(v)))


def step_sizes(raw_ref, bias_ref):
    return softplus(raw_ref[...] + bias_ref[...])


def lanes(column, width=CHUNK):
    return jnp.broadcast_to(column, (column.shape[0], width))


def per_head(rows, matrix):
    heads = rows.shape[0]
    shaped = matrix.reshape(heads, matrix.shape[0] // heads, matrix.shape[1])
    return (shaped * rows[:, None, :]).reshape(matrix.shape)


def head_sums(matrix, heads):
    return jnp.sum(matrix.reshape(heads, matrix.shape[0] // heads, matrix.shape[1]), axis=1)


def pair_blocks(first, second):
    zero = jnp.zeros_like(first)
    return jnp.concatenate(
        [jnp.concatenate([first, zero], axis=1), jnp.concatenate([zero, second], axis=1)], axis=0
    )


def triangle(lower):
    row = lax.broadcasted_iota(jnp.int32, (CHUNK, CHUNK), 0)
    col = lax.broadcasted_iota(jnp.int32, (CHUNK, CHUNK), 1)
    return (row >= col) if lower else (row <= col)


def span_of(c):
    return slice(c * CHUNK, (c + 1) * CHUNK)


def states_kernel(x_ref, g_ref, raw_ref, bias_ref, rate_ref, b_ref, c_ref,
                  xt_ref, gt_ref, dt_ref, cum_ref, end_ref, s_ref, r_ref):
    heads, tokens = raw_ref.shape
    chunks = tokens // CHUNK
    dt = step_sizes(raw_ref, bias_ref)
    dt_ref[...] = dt
    log_decay = -rate_ref[...] * dt
    ones = triangle(False).astype(F32)
    xt_ref[...] = x_ref[...].T
    gt_ref[...] = g_ref[...].T
    cums = [jnp.dot(log_decay[:, span_of(c)], ones, precision=HIGH) for c in range(chunks)]
    ends = [lanes(cum[:, CHUNK - 1:]) for cum in cums]
    total = ends[0]
    for end in ends[1:]:
        total = total + end
    end_ref[...] = total
    state = None
    for c in range(chunks):
        cum_ref[:, span_of(c)] = cums[c]
        weight = jnp.exp(ends[c] - cums[c]) * dt[:, span_of(c)]
        high, low = split(per_head(weight, xt_ref[:, span_of(c)].astype(F32)))
        b = b_ref[span_of(c), :]
        added = mm(high, b) + mm(low, b)
        state = added if state is None else per_head(jnp.exp(ends[c]), state) + added
        s_ref[c] = state
    back = None
    for c in reversed(range(chunks)):
        high, low = split(per_head(jnp.exp(cums[c]), gt_ref[:, span_of(c)].astype(F32)))
        cc = c_ref[span_of(c), :]
        added = mm(high, cc) + mm(low, cc)
        back = added if back is None else per_head(jnp.exp(ends[c]), back) + added
        r_ref[c] = back


def within_kernel(x_ref, xt_ref, gt_ref, dt_ref, cum_ref, b_ref, c_ref,
                  dxt_ref, row_ref, col_ref, dg_ref):
    heads, tokens = dt_ref.shape
    size = xt_ref.shape[0] // heads
    group = pl.program_id(0)
    causal = triangle(False)

    @pl.when(group == 0)
    def _():
        dg_ref[...] = jnp.zeros_like(dg_ref)

    def one_chunk(c, carry):
        at = pl.ds(pl.multiple_of(c * CHUNK, CHUNK), CHUNK)
        scores = mm_nt(b_ref[at, :], c_ref[at, :])
        cum = cum_ref[:, at]
        shifted = (cum - jnp.log(dt_ref[:, at])).T
        total = jnp.zeros((CHUNK, CHUNK), F32)
        rows, cols = [], []
        for pair in range(heads // 2):
            x_pair = x_ref[at, pair * 2 * size:(pair + 1) * 2 * size]
            places = [slice((2 * pair + j) * size, (2 * pair + j + 1) * size) for j in range(2)]
            products = mm(x_pair, pair_blocks(gt_ref[places[0], at], gt_ref[places[1], at]))
            for j in range(2):
                h = 2 * pair + j
                gap = cum[h:h + 1, :] - shifted[:, h:h + 1]
                decay = jnp.exp(jnp.where(causal, gap, -1e30))
                total = total + products[:, j * CHUNK:(j + 1) * CHUNK] * decay
                high, low = split(decay * scores)
                x_h = xt_ref[places[j], at]
                g_h = gt_ref[places[j], at]
                y_h = mm(x_h, high) + mm(x_h, low)
                dx_h = mm_nt(g_h, high) + mm_nt(g_h, low)
                dxt_ref[places[j], at] = dx_h
                rows.append(jnp.sum(y_h * g_h.astype(F32), axis=0, keepdims=True))
                cols.append(jnp.sum(dx_h * x_h.astype(F32), axis=0, keepdims=True))
        row_ref[:, at] = jnp.concatenate(rows, axis=0)
        col_ref[:, at] = jnp.concatenate(cols, axis=0)
        dg_ref[c] += total
        return carry

    lax.fori_loop(0, tokens // CHUNK, one_chunk, 0)


def across_kernel(x_ref, g_ref, xt_ref, gt_ref, raw_ref, bias_ref, rate_ref, skip_ref, dt_ref,
                  cum_ref, s_ref, r_ref, sin_ref, rin_ref, dxt_ref, row_ref, col_ref,
                  b_ref, c_ref, dg_ref,
                  gx_ref, graw_ref, gparam_ref, db_ref, dc_ref):
    heads, tokens = dt_ref.shape
    chunks = tokens // CHUNK
    size = xt_ref.shape[0] // heads
    group = pl.program_id(0)

    @pl.when(group == 0)
    def _():
        for c in range(chunks):
            high, low = split(dg_ref[c])
            db_ref[span_of(c), :] = mm(high, c_ref[span_of(c), :]) + mm(low, c_ref[span_of(c), :])
            high, low = split(dg_ref[c].T)
            dc_ref[span_of(c), :] = mm(high, b_ref[span_of(c), :]) + mm(low, b_ref[span_of(c), :])

    ends = [lanes(cum_ref[:, (c + 1) * CHUNK - 1:(c + 1) * CHUNK]) for c in range(chunks)]
    before = [jnp.zeros_like(ends[0])]
    for end in ends:
        before.append(before[-1] + end)
    after = [jnp.zeros_like(ends[0])]
    for end in reversed(ends):
        after.insert(0, after[0] + end)
    skip = lanes(skip_ref[...])
    rate = lanes(rate_ref[...])
    rows, cols, crossed = [], [], None
    for c in range(chunks):
        at = span_of(c)
        cum, dt = cum_ref[:, at], dt_ref[:, at]
        reach = jnp.exp(cum)
        weight = jnp.exp(ends[c] - cum) * dt
        state = per_head(jnp.exp(before[c]), sin_ref[...])
        if c > 0:
            state = state + s_ref[c - 1]
        back = per_head(jnp.exp(after[c + 1]), rin_ref[...])
        if c < chunks - 1:
            back = back + r_ref[c + 1]
        s_high, s_low = split(state)
        r_high, r_low = split(back)
        b, cc = b_ref[at, :], c_ref[at, :]
        xt, gt = xt_ref[:, at].astype(F32), gt_ref[:, at].astype(F32)
        y = mm_nt(s_high, cc) + mm_nt(s_low, cc)
        rows.append(row_ref[:, at] + head_sums(y * gt, heads) * reach)
        dx = per_head(weight, mm_nt(r_high, b) + mm_nt(r_low, b))
        cols.append(col_ref[:, at] + head_sums(dx * xt, heads))
        product = head_sums(xt * gt, heads)
        crossed = product if crossed is None else crossed + product
        dx = dx + dxt_ref[:, at] + per_head(skip, gt)
        gx_ref[at, :] = dx.astype(BF16).T
        reach_t, weight_t = reach.T, weight.T
        dc = jnp.zeros((CHUNK, cc.shape[1]), F32)
        db = jnp.zeros((CHUNK, cc.shape[1]), F32)
        width = cc.shape[1]
        for pair in range(heads // 2):
            wide = slice(pair * 2 * size, (pair + 1) * 2 * size)
            one = slice(2 * pair * size, (2 * pair + 1) * size)
            two = slice((2 * pair + 1) * size, (2 * pair + 2) * size)
            g_pair, x_pair = g_ref[at, wide], x_ref[at, wide]
            gs = (mm(g_pair, pair_blocks(s_high[one], s_high[two]))
                  + mm(g_pair, pair_blocks(s_low[one], s_low[two])))
            xr = (mm(x_pair, pair_blocks(r_high[one], r_high[two]))
                  + mm(x_pair, pair_blocks(r_low[one], r_low[two])))
            for j in range(2):
                h = 2 * pair + j
                dc = dc + gs[:, j * width:(j + 1) * width] * reach_t[:, h:h + 1]
                db = db + xr[:, j * width:(j + 1) * width] * weight_t[:, h:h + 1]
        dc_ref[at, :] += dc
        db_ref[at, :] += db
    last = s_ref[chunks - 1] + per_head(jnp.exp(before[chunks]), sin_ref[...])
    beyond = lanes(jnp.sum(head_sums(last * rin_ref[...], heads), axis=1, keepdims=True))
    suffix = triangle(True).astype(F32)
    g_rate = jnp.zeros((heads, 1), F32)
    g_bias = jnp.zeros((heads, 1), F32)
    for c in reversed(range(chunks)):
        at = span_of(c)
        change = rows[c] - cols[c]
        d_log = jnp.dot(change, suffix, precision=HIGH) + beyond
        beyond = beyond + lanes(jnp.sum(change, axis=1, keepdims=True))
        dt = dt_ref[:, at]
        g_dt = cols[c] / dt - rate * d_log
        v = raw_ref[:, at] + bias_ref[...]
        g_raw = g_dt / (1.0 + jnp.exp(-v))
        graw_ref[:, at] = g_raw
        g_rate = g_rate - jnp.sum(dt * d_log, axis=1, keepdims=True)
        g_bias = g_bias + jnp.sum(g_raw, axis=1, keepdims=True)
    g_skip = jnp.sum(crossed, axis=1, keepdims=True)
    lane = lax.broadcasted_iota(jnp.int32, (heads, CHUNK), 1)
    gparam_ref[...] = jnp.where(lane == 0, g_rate, jnp.where(lane == 1, g_skip, g_bias))


def hypercube_shift(value, axis, distance):
    peers = lax.axis_size(axis)
    return lax.ppermute(value, axis, [(i, i ^ distance) for i in range(peers)])


def carried(span, states, adjoints, axis):
    peers, place = lax.axis_size(axis), lax.axis_index(axis)
    heads = span.shape[0]
    half = heads // 2
    odd = (place % 2) == 1

    def halves(whole):
        first, second = whole[:half], whole[half:]
        return jnp.where(odd, second, first), jnp.where(odd, first, second)

    def scale(log):
        return jnp.exp(log)[:, None, None]

    s_mine, s_theirs = halves(states)
    r_mine, r_theirs = halves(adjoints)
    other = hypercube_shift(span, axis, 1)
    s_got, r_got = hypercube_shift((s_theirs, r_theirs), axis, 1)
    log_mine, log_got = halves(span)[0], halves(other)[0]
    log_even, log_odd = jnp.where(odd, log_got, log_mine), jnp.where(odd, log_mine, log_got)
    s_even, s_odd = jnp.where(odd, s_got, s_mine), jnp.where(odd, s_mine, s_got)
    r_even, r_odd = jnp.where(odd, r_got, r_mine), jnp.where(odd, r_mine, r_got)
    s_all = scale(log_odd) * s_even + s_odd
    r_all = r_even + scale(log_even) * r_odd
    log_all = log_even + log_odd
    s_pre, r_pre = jnp.zeros_like(s_all), jnp.zeros_like(r_all)
    s_log, r_log = jnp.zeros_like(log_all), jnp.zeros_like(log_all)
    distance = 2
    while distance < peers:
        upper = (place // distance) % 2 == 1
        final = distance * 2 >= peers
        log_new = hypercube_shift(log_all, axis, distance)
        if final:
            s_new = r_new = hypercube_shift(jnp.where(upper, r_all, s_all), axis, distance)
        else:
            s_new, r_new = hypercube_shift((s_all, r_all), axis, distance)
        s_pre = jnp.where(upper, s_pre + scale(s_log) * s_new, s_pre)
        r_pre = jnp.where(upper, r_pre, r_pre + scale(r_log) * r_new)
        if not final:
            s_log = jnp.where(upper, s_log + log_new, s_log)
            r_log = jnp.where(upper, r_log, r_log + log_new)
            s_all = jnp.where(upper, scale(log_all) * s_new + s_all, scale(log_new) * s_all + s_new)
            r_all = jnp.where(upper, r_new + scale(log_new) * r_all, r_all + scale(log_all) * r_new)
            log_all = log_all + log_new
        distance *= 2
    s_for_odd = s_even + scale(log_even) * s_pre
    r_for_even = r_odd + scale(log_odd) * r_pre
    s_keep, s_give = jnp.where(odd, s_for_odd, s_pre), jnp.where(odd, s_pre, s_for_odd)
    r_keep, r_give = jnp.where(odd, r_pre, r_for_even), jnp.where(odd, r_for_even, r_pre)
    s_back, r_back = hypercube_shift((s_give, r_give), axis, 1)

    def whole(keep, back):
        return jnp.concatenate([jnp.where(odd, back, keep), jnp.where(odd, keep, back)], axis=0)

    return whole(s_keep, s_back), whole(r_keep, r_back)


def on_device(tokens_x, raw_dt, in_b, in_c, decay_rate, skip_gain, step_bias, grad_y):
    heads, tokens = raw_dt.shape
    width = tokens_x.shape[1]
    size = width // heads
    state = in_b.shape[1]
    chunks = tokens // CHUNK
    wide = GROUP * size
    grid = (heads // GROUP,)

    def shape(*dims, dtype=F32):
        return jax.ShapeDtypeStruct(dims, dtype)

    tokens_by_wide = pl.BlockSpec((tokens, wide), lambda i: (0, i))
    wide_by_tokens = pl.BlockSpec((wide, tokens), lambda i: (i, 0))
    head_rows = pl.BlockSpec((GROUP, tokens), lambda i: (i, 0))
    head_lanes = pl.BlockSpec((GROUP, CHUNK), lambda i: (i, 0))
    head_column = pl.BlockSpec((GROUP, 1), lambda i: (i, 0))
    projection = pl.BlockSpec((tokens, state), lambda i: (0, 0))
    state_block = pl.BlockSpec((wide, state), lambda i: (i, 0))
    state_blocks = pl.BlockSpec((chunks, wide, state), lambda i: (0, i, 0))
    score_blocks = pl.BlockSpec((chunks, CHUNK, CHUNK), lambda i: (0, 0, 0))
    bias, rate, skip = (v.reshape(heads, 1) for v in (step_bias, decay_rate, skip_gain))

    xt, gt, dt, cum, end, s_loc, r_loc = pl.pallas_call(
        states_kernel,
        grid=grid,
        in_specs=[tokens_by_wide, tokens_by_wide, head_rows, head_column, head_column,
                  projection, projection],
        out_specs=[wide_by_tokens, wide_by_tokens, head_rows, head_rows, head_lanes,
                   state_blocks, state_blocks],
        out_shape=[shape(width, tokens, dtype=BF16), shape(width, tokens, dtype=BF16),
                   shape(heads, tokens), shape(heads, tokens), shape(heads, CHUNK),
                   shape(chunks, width, state), shape(chunks, width, state)],
        compiler_params=PARAMS,
        name="states",
    )(tokens_x, grad_y, raw_dt, bias, rate, in_b, in_c)

    s_in, r_in = carried(
        end[:, 0],
        s_loc[chunks - 1].reshape(heads, size, state),
        r_loc[0].reshape(heads, size, state),
        "ctx",
    )

    dxt, row, col, dg = pl.pallas_call(
        within_kernel,
        grid=grid,
        in_specs=[tokens_by_wide, wide_by_tokens, wide_by_tokens, head_rows, head_rows,
                  projection, projection],
        out_specs=[wide_by_tokens, head_rows, head_rows, score_blocks],
        out_shape=[shape(width, tokens), shape(heads, tokens), shape(heads, tokens),
                   shape(chunks, CHUNK, CHUNK)],
        compiler_params=PARAMS,
        cost_estimate=pl.CostEstimate(
            flops=24 * width * tokens * CHUNK,
            bytes_accessed=14 * width * tokens,
            transcendentals=heads * tokens * CHUNK,
        ),
        name="within",
    )(tokens_x, xt, gt, dt, cum, in_b, in_c)

    grad_x, grad_raw, params, grad_b, grad_c = pl.pallas_call(
        across_kernel,
        grid=grid,
        in_specs=[tokens_by_wide, tokens_by_wide, wide_by_tokens, wide_by_tokens, head_rows,
                  head_column, head_column, head_column, head_rows, head_rows, state_blocks,
                  state_blocks, state_block, state_block, wide_by_tokens, head_rows, head_rows,
                  projection, projection, score_blocks],
        out_specs=[tokens_by_wide, head_rows, head_lanes, projection, projection],
        out_shape=[shape(tokens, width, dtype=BF16), shape(heads, tokens), shape(heads, CHUNK),
                   shape(tokens, state), shape(tokens, state)],
        compiler_params=PARAMS,
        name="across",
    )(tokens_x, grad_y, xt, gt, raw_dt, bias, rate, skip, dt, cum, s_loc, r_loc,
      s_in.reshape(width, state), r_in.reshape(width, state), dxt, row, col, in_b, in_c, dg)

    grad_b, grad_c = lax.psum((grad_b, grad_c), "head")
    params = params[:, :3]
    distance = 1
    while distance < lax.axis_size("ctx"):
        params = params + hypercube_shift(params, "ctx", distance)
        distance *= 2
    return (grad_x, grad_raw, grad_b, grad_c, params[:, 0], params[:, 1], params[:, 2])


def solution(mesh):
    placed = (
        P("ctx", "head"),
        P("head", "ctx"),
        P("ctx", None),
        P("ctx", None),
        P("head"),
        P("head"),
        P("head"),
        P("ctx", "head"),
    )
    return jax.shard_map(
        on_device,
        mesh=mesh,
        in_specs=placed,
        out_specs=(
            P("ctx", "head"),
            P("head", "ctx"),
            P("ctx", None),
            P("ctx", None),
            P("head"),
            P("head"),
            P("head"),
        ),
        check_vma=False,
    )
```

profile of v0, /device:TPU:0, one launch (start us, length us, event | category | flops | bytes accessed | tf_op | source)
XLA Modules:
  0.0 155.4 jit_solution(4521968887609684235)
XLA Ops:
  7.2 1.3 copy.21.rate_ref
  8.5 1.3 copy.20.bias_ref
  9.9 8.6 %states.1 = (bf16[2048,512]{1,0:T(8,128)(2,1)}, bf16[2048,512]{1,0:T(8,128)(2,1)}, f32[32,512]{1,0:T(8,128)}, f32[32,512]{1,0:T(8,128)}, f32[32,128]{1,0:T(8,128...) custom-call(bf16[512,2048]{1,0:T(8,128)(2,1)} %x_ref.5, bf16[512,2048]{1,0:T(8,128)(2,1)} %g_ref.3, ...), custom_call_target="tpu_custom_call" | custom-call | tf_op jit(solution)/shard_map/states/pallas_call | solution.py:321
  18.4 0.9 slice_reduce_fusion.3
  19.9 1.3 slice_select_fusion.2
  21.3 1.3 slice_select_fusion
  23.3 0.9 select_add_fusion
  24.2 2.5 %collective-permute-start.2 = (f32[16,64,128]{2,1,0:T(8,128)}, f32[16,64,128]{2,1,0:T(8,128)S(1)}, u32[]{:S(2)}, u32[]{:S(2)}) collective-permute-start(f32[16,64,128]{2,1,0:T(8,128)} %select_add_fusion), channel_id=1, source_target_pairs={{0,8},{4,12},{8,0},{12,4},{16,24},{20,28},{24,16},{28,20},{1,9},{5... | collective-permute-start | bytes 1572872 | tf_op jit(solution)/shard_map/ppermute | solution.py:239
  26.7 0.9 multiply_add_fusion.2
  27.7 0.7 collective-permute-start.5
  28.4 1.3 collective-permute-start.3
  29.7 21.1 %collective-permute-done.3 = f32[16]{0:T(128)S(1)} collective-permute-done((f32[16]{0:T(128)S(1)}, f32[16]{0:T(128)S(1)}, u32[]{:S(2)}, u32[]{:S(2)}) %collective-permute-start.3) | collective-permute-done | bytes 96 | tf_op jit(solution)/shard_map/ppermute | solution.py:239
  50.9 1.5 select_select_fusion
  52.3 1.8 %collective-permute-start.6 = (f32[16,64,128]{2,1,0:T(8,128)S(1)}, f32[16,64,128]{2,1,0:T(8,128)S(1)}, u32[]{:S(2)}, u32[]{:S(2)}) collective-permute-start(f32[16,64,128]{2,1,0:T(8,128)S(1)} %select_select_fusion), channel_id=1, source_target_pairs={{0,16},{4,20},{8,24},{12,28},{16,0},{20,4},{24,8},{28,12},{1,17},{... | collective-permute-start | bytes 1572872 | tf_op jit(solution)/shard_map/ppermute | solution.py:239
  54.2 11.9 %collective-permute-done.6 = f32[16,64,128]{2,1,0:T(8,128)S(1)} collective-permute-done((f32[16,64,128]{2,1,0:T(8,128)S(1)}, f32[16,64,128]{2,1,0:T(8,128)S(1)}, u32[]{:S(2)}, u32[]{:S(2)}) %collective-permute-start.6) | collective-permute-done | bytes 524320 | tf_op jit(solution)/shard_map/ppermute | solution.py:239
  66.0 0.8 copy-done
  66.8 1.3 fusion.1
  69.4 16.5 %within.1 = (f32[2048,512]{1,0:T(8,128)}, f32[32,512]{1,0:T(8,128)}, f32[32,512]{1,0:T(8,128)}, f32[4,128,128]{2,1,0:T(8,128)}) custom-call(bf16[512,2048]{1,0:T(8,128)(2,1)} %x_ref.5, bf16[2048,512]{1,0:T(8,128)(2,1)} %get-tuple-element.23.xt_ref, bf16[2048,512]{1,0:T(8,128)(2,1)} %get-tuple-element.24.gt_ref, f32[32,512]{1,0:T(8,128)} %get-tuple-element.25.dt_ref, ...), custom_call_target="tpu_custom_call" | custom-call | flops 3221225472 | bytes 14680064 | tf_op jit(solution)/shard_map/within/pallas_call | solution.py:342
  86.3 1.4 broadcast_select_fusion
  87.7 1.1 pad_maximum_fusion.1
  88.8 1.1 pad_maximum_fusion
  89.9 15.3 %across.1 = (bf16[512,2048]{1,0:T(8,128)(2,1)}, f32[32,512]{1,0:T(8,128)}, f32[32,128]{1,0:T(8,128)}, f32[512,128]{1,0:T(8,128)}, f32[512,128]{1,0:T(8,128)}) custom-call(bf16[512,2048]{1,0:T(8,128)(2,1)} %x_ref.5, bf16[512,2048]{1,0:T(8,128)(2,1)} %g_ref.3, bf16[2048,512]{1,0:T(8,128)(2,1)} %get-tuple-element.23.xt_ref, ...), custom_call_target="tpu_custom_call" | custom-call | tf_op jit(solution)/shard_map/across/pallas_call | solution.py:359
  105.3 1.4 collective-permute-done.9
  106.7 0.7 slice_add_fusion
  107.4 1.5 collective-permute-start.10
  108.8 2.3 %collective-permute-done.10 = f32[32,3]{1,0:T(8,128)S(1)} collective-permute-done((f32[32,3]{1,0:T(8,128)S(1)}, f32[32,3]{1,0:T(8,128)S(1)}, u32[]{:S(2)}, u32[]{:S(2)}) %collective-permute-start.10) | collective-permute-done | bytes 416 | tf_op jit(solution)/shard_map/ppermute | solution.py:239
  111.1 1.5 collective-permute-start.11
  112.6 2.2 %collective-permute-done.11 = f32[32,3]{1,0:T(8,128)S(1)} collective-permute-done((f32[32,3]{1,0:T(8,128)S(1)}, f32[32,3]{1,0:T(8,128)S(1)}, u32[]{:S(2)}, u32[]{:S(2)}) %collective-permute-start.11) | collective-permute-done | bytes 416 | tf_op jit(solution)/shard_map/ppermute | solution.py:239
  114.9 0.7 slice_reduce_fusion
  115.6 29.6 %all-reduce.3.cloned.1.call-done = (f32[512,128]{1,0:T(8,128)}, f32[512,128]{1,0:T(8,128)}) async-done(((f32[512,128]{1,0:T(8,128)}, f32[512,128]{1,0:T(8,128)}), (f32[512,128]{1,0:T(8,128)}, f32[512,128]{1,0:T(8,128)})) %all-reduce.3.cloned.1.call-update) | async-done | bytes 524304 | tf_op jit(solution)/shard_map/psum | solution.py:374
  145.2 1.7 %copy.27 = f32[512,128]{1,0:T(8,128)} copy(f32[512,128]{1,0:T(8,128)} %get-tuple-element.67) | data formatting | bytes 524288
  146.9 1.7 %copy.28 = f32[512,128]{1,0:T(8,128)} copy(f32[512,128]{1,0:T(8,128)} %get-tuple-element.68) | data formatting | bytes 524288
  (31 shorter events, 3.2 us)
Async XLA Ops:
  7.2 138.0 %all-reduce.3.cloned.1.call-start = ((), (), s32[]{:S(2)}) async-start(), calls=%async_computation | async-start | bytes 1048576 | tf_op jit(solution)/shard_map/psum | solution.py:374
  18.4 4.6 %copy-start.2 = (f32[32,128]{1,0:T(8,128)S(1)}, f32[32,128]{1,0:T(8,128)}, u32[]{:S(2)}) copy-start(f32[32,128]{1,0:T(8,128)} %get-tuple-element.29) | copy-start | bytes 49156
  19.3 3.9 %collective-permute-start = (f32[32]{0:T(128)S(1)}, f32[32]{0:T(128)S(1)}, u32[]{:S(2)}, u32[]{:S(2)}) collective-permute-start(f32[32]{0:T(128)S(1)} %slice_reduce_fusion.3), channel_id=1, source_target_pairs={{0,4},{4,0},{8,12},{12,8},{16,20},{20,16},{24,28},{28,24},{1,5},{5... | collective-permute-start | bytes 392 | tf_op jit(solution)/shard_map/ppermute | solution.py:239
  21.2 2.1 %collective-permute-start.1 = (f32[16,64,128]{2,1,0:T(8,128)S(1)}, f32[16,64,128]{2,1,0:T(8,128)S(1)}, u32[]{:S(2)}, u32[]{:S(2)}) collective-permute-start(f32[16,64,128]{2,1,0:T(8,128)S(1)} %bitcast.19), channel_id=1, source_target_pairs={{0,4},{4,0},{8,12},{12,8},{16,20},{20,16},{24,28},{28,24},{1,5},{5... | collective-permute-start | bytes 1572872 | tf_op jit(solution)/shard_map/ppermute | solution.py:239
  22.5 4.2 %collective-permute-start.4 = (f32[16,64,128]{2,1,0:T(8,128)S(1)}, f32[16,64,128]{2,1,0:T(8,128)S(1)}, u32[]{:S(2)}, u32[]{:S(2)}) collective-permute-start(f32[16,64,128]{2,1,0:T(8,128)S(1)} %bitcast.18), channel_id=1, source_target_pairs={{0,4},{4,0},{8,12},{12,8},{16,20},{20,16},{24,28},{28,24},{1,5},{5... | collective-permute-start | bytes 1572872 | tf_op jit(solution)/shard_map/ppermute | solution.py:239
  24.2 26.6 %collective-permute-start.2 = (f32[16,64,128]{2,1,0:T(8,128)}, f32[16,64,128]{2,1,0:T(8,128)S(1)}, u32[]{:S(2)}, u32[]{:S(2)}) collective-permute-start(f32[16,64,128]{2,1,0:T(8,128)} %select_add_fusion), channel_id=1, source_target_pairs={{0,8},{4,12},{8,0},{12,4},{16,24},{20,28},{24,16},{28,20},{1,9},{5... | collective-permute-start | bytes 1572872 | tf_op jit(solution)/shard_map/ppermute | solution.py:239
  26.7 42.0 %copy-start.3 = (f32[32]{0:T(128)S(1)}, f32[32]{0:T(128)}, u32[]{:S(2)}) copy-start(f32[32]{0:T(128)} %param.13) | copy-start | bytes 388
  27.7 23.2 %collective-permute-start.5 = (f32[16,64,128]{2,1,0:T(8,128)}, f32[16,64,128]{2,1,0:T(8,128)S(1)}, u32[]{:S(2)}, u32[]{:S(2)}) collective-permute-start(f32[16,64,128]{2,1,0:T(8,128)} %multiply_add_fusion.2), channel_id=1, source_target_pairs={{0,8},{4,12},{8,0},{12,4},{16,24},{20,28},{24,16},{28,20},{1,9},{5... | collective-permute-start | bytes 1572872 | tf_op jit(solution)/shard_map/ppermute | solution.py:239
  28.4 22.4 %collective-permute-start.3 = (f32[16]{0:T(128)S(1)}, f32[16]{0:T(128)S(1)}, u32[]{:S(2)}, u32[]{:S(2)}) collective-permute-start(f32[16]{0:T(128)S(1)} %get-tuple-element.49), channel_id=1, source_target_pairs={{0,8},{4,12},{8,0},{12,4},{16,24},{20,28},{24,16},{28,20},{1,9},{5... | collective-permute-start | bytes 200 | tf_op jit(solution)/shard_map/ppermute | solution.py:239
  52.3 13.7 %collective-permute-start.6 = (f32[16,64,128]{2,1,0:T(8,128)S(1)}, f32[16,64,128]{2,1,0:T(8,128)S(1)}, u32[]{:S(2)}, u32[]{:S(2)}) collective-permute-start(f32[16,64,128]{2,1,0:T(8,128)S(1)} %select_select_fusion), channel_id=1, source_target_pairs={{0,16},{4,20},{8,24},{12,28},{16,0},{20,4},{24,8},{28,12},{1,17},{... | collective-permute-start | bytes 1572872 | tf_op jit(solution)/shard_map/ppermute | solution.py:239
  66.0 0.8 copy-start
  68.2 17.7 %collective-permute-start.8 = (f32[16,64,128]{2,1,0:T(8,128)}, f32[16,64,128]{2,1,0:T(8,128)}, u32[]{:S(2)}, u32[]{:S(2)}) collective-permute-start(f32[16,64,128]{2,1,0:T(8,128)} %get-tuple-element.58), channel_id=1, source_target_pairs={{0,4},{4,0},{8,12},{12,8},{16,20},{20,16},{24,28},{28,24},{1,5},{5... | collective-permute-start | bytes 1572872 | tf_op jit(solution)/shard_map/ppermute | solution.py:239
  68.2 17.7 %collective-permute-start.7 = (f32[16,64,128]{2,1,0:T(8,128)}, f32[16,64,128]{2,1,0:T(8,128)}, u32[]{:S(2)}, u32[]{:S(2)}) collective-permute-start(f32[16,64,128]{2,1,0:T(8,128)} %get-tuple-element.59), channel_id=1, source_target_pairs={{0,4},{4,0},{8,12},{12,8},{16,20},{20,16},{24,28},{28,24},{1,5},{5... | collective-permute-start | bytes 1572872 | tf_op jit(solution)/shard_map/ppermute | solution.py:239
  69.4 16.5 %copy-start.1 = (f32[16,64,128]{2,1,0:T(8,128)S(1)}, f32[16,64,128]{2,1,0:T(8,128)}, u32[]{:S(2)}) copy-start(f32[16,64,128]{2,1,0:T(8,128)} %copy-done) | copy-start | bytes 1572868
  105.2 1.5 collective-permute-start.9
  107.4 3.7 %collective-permute-start.10 = (f32[32,3]{1,0:T(8,128)S(1)}, f32[32,3]{1,0:T(8,128)S(1)}, u32[]{:S(2)}, u32[]{:S(2)}) collective-permute-start(f32[32,3]{1,0:T(8,128)S(1)} %slice_add_fusion), channel_id=1, source_target_pairs={{0,8},{4,12},{8,0},{12,4},{16,24},{20,28},{24,16},{28,20},{1,9},{5... | collective-permute-start | bytes 1160 | tf_op jit(solution)/shard_map/ppermute | solution.py:239
  111.1 3.7 %collective-permute-start.11 = (f32[32,3]{1,0:T(8,128)S(1)}, f32[32,3]{1,0:T(8,128)S(1)}, u32[]{:S(2)}, u32[]{:S(2)}) collective-permute-start(f32[32,3]{1,0:T(8,128)S(1)} %add.73), channel_id=1, source_target_pairs={{0,16},{4,20},{8,24},{12,28},{16,0},{20,4},{24,8},{28,12},{1,17},{... | collective-permute-start | bytes 1160 | tf_op jit(solution)/shard_map/ppermute | solution.py:239
Sparse Core Ops, SparseCore 0:
  105.3 39.8 all-reduce.2
where the time goes:
time: 156 us; the launch traced here: 155 us
  waiting for transfers between devices  68.5 us (44%)
  Pallas kernels  40.3 us (26%)
  between operations  14.1 us (9%)
  other arithmetic  12.1 us (8%)
  starting transfers between devices  11.2 us (7%)
  local copies, waits for them, and re-layouts  9.12 us (6%)
    ppermute x12, waiting for transfers between devices, hypercube_shift(): return lax.ppermute(value, axis, [(i, i ^ distance) for i in range(peers)])  38.9 us
    psum x1, waiting for transfers between devices, on_device(): grad_b, grad_c = lax.psum((grad_b, grad_c), 'head')  29.6 us
    pallas_call x1, Pallas kernels, on_device(): pl.pallas_call(within_kernel, grid=grid, in_specs=[tokens_by_wide, wide_b...  16.5 us
    pallas_call x1, Pallas kernels, on_device(): pl.pallas_call(across_kernel, grid=grid, in_specs=[tokens_by_wide, tokens...  15.3 us
    ppermute x12, starting transfers between devices, hypercube_shift(): return lax.ppermute(value, axis, [(i, i ^ distance) for i in range(peers)])  11.1 us
    pallas_call x1, Pallas kernels, on_device(): pl.pallas_call(states_kernel, grid=grid, in_specs=[tokens_by_wide, tokens...  8.56 us
    unnamed x10, local copies, waits for them, and re-layouts  4.14 us
    reshape x3, local copies, waits for them, and re-layouts, on_device(): v.reshape(heads, 1)  3.35 us
  transfers between devices with their start and end apart: 13, of which 6 were waited for; matrix products, arithmetic and copies ran while one was open for 4% of the time, Pallas kernels for 11%

commit v1 on v0

--- a/solution.py
+++ b/solution.py
@@ -4,6 +4,7 @@
 from jax.experimental import pallas as pl
 from jax.experimental.pallas import tpu as pltpu
 from jax.sharding import PartitionSpec as P
+
 
 CHUNK = 128
 GROUP = 8
@@ -31,10 +32,6 @@
     return jnp.maximum(v, 0.0) + jnp.log1p(jnp.exp(-jnp.abs(v)))
 
 
-def step_sizes(raw_ref, bias_ref):
-    return softplus(raw_ref[...] + bias_ref[...])
-
-
 def lanes(column, width=CHUNK):
     return jnp.broadcast_to(column, (column.shape[0], width))
 
@@ -66,13 +63,13 @@
     return slice(c * CHUNK, (c + 1) * CHUNK)
 
 
-def states_kernel(x_ref, g_ref, raw_ref, bias_ref, rate_ref, b_ref, c_ref,
+def states_kernel(x_ref, g_ref, raw_ref, knob_ref, b_ref, c_ref,
                   xt_ref, gt_ref, dt_ref, cum_ref, end_ref, s_ref, r_ref):
-    heads, tokens = raw_ref.shape
+    _, tokens = raw_ref.shape
     chunks = tokens // CHUNK
-    dt = step_sizes(raw_ref, bias_ref)
+    dt = softplus(raw_ref[...] + knob_ref[:, 0:1])
     dt_ref[...] = dt
-    log_decay = -rate_ref[...] * dt
+    log_decay = -knob_ref[:, 1:2] * dt
     ones = triangle(False).astype(F32)
     xt_ref[...] = x_ref[...].T
     gt_ref[...] = g_ref[...].T
@@ -143,10 +140,11 @@
     lax.fori_loop(0, tokens // CHUNK, one_chunk, 0)
 
 
-def across_kernel(x_ref, g_ref, xt_ref, gt_ref, raw_ref, bias_ref, rate_ref, skip_ref, dt_ref,
-                  cum_ref, s_ref, r_ref, sin_ref, rin_ref, dxt_ref, row_ref, col_ref,
+def across_kernel(x_ref, g_ref, xt_ref, gt_ref, raw_ref, knob_ref, dt_ref, cum_ref,
+                  s_ref, r_ref, sin_ref, rin_ref, dxt_ref, row_ref, col_ref,
                   b_ref, c_ref, dg_ref,
-                  gx_ref, graw_ref, gparam_ref, db_ref, dc_ref):
+                  gx_ref, graw_ref, gparam_ref, dbc_ref):
+    db_ref, dc_ref = dbc_ref.at[0], dbc_ref.at[1]
     heads, tokens = dt_ref.shape
     chunks = tokens // CHUNK
     size = xt_ref.shape[0] // heads
@@ -167,8 +165,8 @@
     after = [jnp.zeros_like(ends[0])]
     for end in reversed(ends):
         after.insert(0, after[0] + end)
-    skip = lanes(skip_ref[...])
-    rate = lanes(rate_ref[...])
+    skip = lanes(knob_ref[:, 2:3])
+    rate = lanes(knob_ref[:, 1:2])
     rows, cols, crossed = [], [], None
     for c in range(chunks):
         at = span_of(c)
@@ -224,7 +222,7 @@
         beyond = beyond + lanes(jnp.sum(change, axis=1, keepdims=True))
         dt = dt_ref[:, at]
         g_dt = cols[c] / dt - rate * d_log
-        v = raw_ref[:, at] + bias_ref[...]
+        v = raw_ref[:, at] + knob_ref[:, 0:1]
         g_raw = g_dt / (1.0 + jnp.exp(-v))
         graw_ref[:, at] = g_raw
         g_rate = g_rate - jnp.sum(dt * d_log, axis=1, keepdims=True)
@@ -273,7 +271,8 @@
         if final:
             s_new = r_new = hypercube_shift(jnp.where(upper, r_all, s_all), axis, distance)
         else:
-            s_new, r_new = hypercube_shift((s_all, r_all), axis, distance)
+            s_new = hypercube_shift(s_all, axis, distance)
+            r_new = hypercube_shift(r_all, axis, distance)
         s_pre = jnp.where(upper, s_pre + scale(s_log) * s_new, s_pre)
         r_pre = jnp.where(upper, r_pre, r_pre + scale(r_log) * r_new)
         if not final:
@@ -295,6 +294,25 @@
     return whole(s_keep, s_back), whole(r_keep, r_back)
 
 
+def reduce_over(value, axis):
+    peers, place = lax.axis_size(axis), lax.axis_index(axis)
+    rows = value.shape[1] // peers
+
+    def shift(piece, step):
+        return lax.ppermute(piece, axis, [(i, (i + step) % peers) for i in range(peers)])
+
+    def piece_of(owner):
+        return lax.dynamic_slice_in_dim(value, owner * rows, rows, axis=1)
+
+    got = [shift(piece_of((place + step) % peers), step) for step in range(1, peers)]
+    total = piece_of(place)
+    for piece in got:
+        total = total + piece
+    every = jnp.stack([total] + [shift(total, step) for step in range(1, peers)])
+    ordered = [every[(place - owner) % peers] for owner in range(peers)]
+    return [jnp.concatenate([piece[k] for piece in ordered], axis=0) for k in range(2)]
+
+
 def on_device(tokens_x, raw_dt, in_b, in_c, decay_rate, skip_gain, step_bias, grad_y):
     heads, tokens = raw_dt.shape
     width = tokens_x.shape[1]
@@ -311,17 +329,18 @@
     wide_by_tokens = pl.BlockSpec((wide, tokens), lambda i: (i, 0))
     head_rows = pl.BlockSpec((GROUP, tokens), lambda i: (i, 0))
     head_lanes = pl.BlockSpec((GROUP, CHUNK), lambda i: (i, 0))
-    head_column = pl.BlockSpec((GROUP, 1), lambda i: (i, 0))
+    head_knobs = pl.BlockSpec((GROUP, 3), lambda i: (i, 0))
     projection = pl.BlockSpec((tokens, state), lambda i: (0, 0))
     state_block = pl.BlockSpec((wide, state), lambda i: (i, 0))
     state_blocks = pl.BlockSpec((chunks, wide, state), lambda i: (0, i, 0))
+    projections = pl.BlockSpec((2, tokens, state), lambda i: (0, 0, 0))
     score_blocks = pl.BlockSpec((chunks, CHUNK, CHUNK), lambda i: (0, 0, 0))
-    bias, rate, skip = (v.reshape(heads, 1) for v in (step_bias, decay_rate, skip_gain))
+    knobs = jnp.stack([step_bias, decay_rate, skip_gain], axis=1)
 
     xt, gt, dt, cum, end, s_loc, r_loc = pl.pallas_call(
         states_kernel,
         grid=grid,
-        in_specs=[tokens_by_wide, tokens_by_wide, head_rows, head_column, head_column,
+        in_specs=[tokens_by_wide, tokens_by_wide, head_rows, head_knobs,
                   projection, projection],
         out_specs=[wide_by_tokens, wide_by_tokens, head_rows, head_rows, head_lanes,
                    state_blocks, state_blocks],
@@ -330,7 +349,7 @@
                    shape(chunks, width, state), shape(chunks, width, state)],
         compiler_params=PARAMS,
         name="states",
-    )(tokens_x, grad_y, raw_dt, bias, rate, in_b, in_c)
+    )(tokens_x, grad_y, raw_dt, knobs, in_b, in_c)
 
     s_in, r_in = carried(
         end[:, 0],
@@ -356,22 +375,22 @@
         name="within",
     )(tokens_x, xt, gt, dt, cum, in_b, in_c)
 
-    grad_x, grad_raw, params, grad_b, grad_c = pl.pallas_call(
+    grad_x, grad_raw, params, grad_bc = pl.pallas_call(
         across_kernel,
         grid=grid,
         in_specs=[tokens_by_wide, tokens_by_wide, wide_by_tokens, wide_by_tokens, head_rows,
-                  head_column, head_column, head_column, head_rows, head_rows, state_blocks,
+                  head_knobs, head_rows, head_rows, state_blocks,
                   state_blocks, state_block, state_block, wide_by_tokens, head_rows, head_rows,
                   projection, projection, score_blocks],
-        out_specs=[tokens_by_wide, head_rows, head_lanes, projection, projection],
+        out_specs=[tokens_by_wide, head_rows, head_lanes, projections],
         out_shape=[shape(tokens, width, dtype=BF16), shape(heads, tokens), shape(heads, CHUNK),
-                   shape(tokens, state), shape(tokens, state)],
+                   shape(2, tokens, state)],
         compiler_params=PARAMS,
         name="across",
-    )(tokens_x, grad_y, xt, gt, raw_dt, bias, rate, skip, dt, cum, s_loc, r_loc,
+    )(tokens_x, grad_y, xt, gt, raw_dt, knobs, dt, cum, s_loc, r_loc,
       s_in.reshape(width, state), r_in.reshape(width, state), dxt, row, col, in_b, in_c, dg)
 
-    grad_b, grad_c = lax.psum((grad_b, grad_c), "head")
+    grad_b, grad_c = reduce_over(grad_bc, "head")
     params = params[:, :3]
     distance = 1
     while distance < lax.axis_size("ctx"):

time: 156 us -> 130 us (0.83)
  waiting for transfers between devices: 68.5 us -> 46 us
  between operations: 14.1 us -> 0.77 us
  starting transfers between devices: 11.2 us -> 23 us
  local copies, waits for them, and re-layouts: 9.12 us -> 4.25 us
  other arithmetic: 12.1 us -> 15.2 us
    psum x1 -> x0, waiting for transfers between devices: 29.6 us -> none  [on_device(): grad_b, grad_c = lax.psum((grad_b, grad_c), 'head')]
    ppermute x0 -> x6, starting transfers between devices: none -> 11.9 us  [shift(): lax.ppermute(piece, axis, [(i, (i + step) % peers) for i in range(peers)])]
    ppermute x0 -> x6, waiting for transfers between devices: none -> 8.47 us  [shift(): lax.ppermute(piece, axis, [(i, (i + step) % peers) for i in range(peers)])]
    reshape x3 -> x0, local copies, waits for them, and re-layouts: 3.35 us -> none  [on_device(): v.reshape(heads, 1)]
    unnamed x10 -> x6, local copies, waits for them, and re-layouts: 4.14 us -> 0.81 us
  transfers between devices with their start and end apart: 13 -> 18, of which waited for: 6 -> 6; matrix products, arithmetic and copies ran while one was open for 4% -> 5% of each run, Pallas kernels for 11% -> 13%
where the time goes in v1:
time: 130 us
  waiting for transfers between devices  46 us (35%)
  Pallas kernels  40.4 us (31%)
  starting transfers between devices  23 us (18%)
  other arithmetic  15.2 us (12%)
  local copies, waits for them, and re-layouts  4.25 us (3%)
    ppermute x12, waiting for transfers between devices, hypercube_shift(): return lax.ppermute(value, axis, [(i, i ^ distance) for i in range(peers)])  37.5 us
    pallas_call x1, Pallas kernels, on_device(): pl.pallas_call(within_kernel, grid=grid, in_specs=[tokens_by_wide, wide_b...  16.5 us
    pallas_call x1, Pallas kernels, on_device(): pl.pallas_call(across_kernel, grid=grid, in_specs=[tokens_by_wide, tokens...  15.5 us
    ppermute x6, starting transfers between devices, shift(): lax.ppermute(piece, axis, [(i, (i + step) % peers) for i in range(peers)])  11.9 us
    ppermute x12, starting transfers between devices, hypercube_shift(): return lax.ppermute(value, axis, [(i, i ^ distance) for i in range(peers)])  11.1 us
    ppermute x6, waiting for transfers between devices, shift(): lax.ppermute(piece, axis, [(i, (i + step) % peers) for i in range(peers)])  8.47 us
    pallas_call x1, Pallas kernels, on_device(): pl.pallas_call(states_kernel, grid=grid, in_specs=[tokens_by_wide, tokens...  8.37 us
    select_n x3, other arithmetic, halves(): return (jnp.where(odd, second, first), jnp.where(odd, first, second))  2.65 us
  transfers between devices with their start and end apart: 18, of which 6 were waited for; matrix products, arithmetic and copies ran while one was open for 5% of the time, Pallas kernels for 13%

profile of v1, /device:TPU:0, one launch (start us, length us, event | category | flops | bytes accessed | tf_op | source)
XLA Modules:
  0.0 129.6 jit_solution(13216403674476270299)
XLA Ops:
  2.0 8.4 %states.1 = (bf16[2048,512]{1,0:T(8,128)(2,1)}, bf16[2048,512]{1,0:T(8,128)(2,1)}, f32[32,512]{1,0:T(8,128)}, f32[32,512]{1,0:T(8,128)}, f32[32,128]{1,0:T(8,128...) custom-call(bf16[512,2048]{1,0:T(8,128)(2,1)} %x_ref.5, bf16[512,2048]{1,0:T(8,128)(2,1)} %g_ref.3, ...), custom_call_target="tpu_custom_call" | custom-call | tf_op jit(solution)/shard_map/states/pallas_call | solution.py:340
  10.4 0.9 slice_reduce_fusion.3
  11.8 1.3 slice_select_fusion
  13.2 1.3 slice_select_fusion.2
  15.3 1.0 multiply_add_fusion.2
  16.2 2.5 %collective-permute-start.5 = (f32[16,64,128]{2,1,0:T(8,128)}, f32[16,64,128]{2,1,0:T(8,128)S(1)}, u32[]{:S(2)}, u32[]{:S(2)}) collective-permute-start(f32[16,64,128]{2,1,0:T(8,128)} %multiply_add_fusion.2), channel_id=1, source_target_pairs={{0,8},{4,12},{8,0},{12,4},{16,24},{20,28},{24,16},{28,20},{1,9},{5... | collective-permute-start | bytes 1572872 | tf_op jit(solution)/shard_map/ppermute | solution.py:237
  18.7 0.9 select_add_fusion
  20.3 1.3 %collective-permute-start.3 = (f32[16]{0:T(128)S(1)}, f32[16]{0:T(128)S(1)}, u32[]{:S(2)}, u32[]{:S(2)}) collective-permute-start(f32[16]{0:T(128)S(1)} %get-tuple-element.45), channel_id=1, source_target_pairs={{0,8},{4,12},{8,0},{12,4},{16,24},{20,28},{24,16},{28,20},{1,9},{5... | collective-permute-start | bytes 200 | tf_op jit(solution)/shard_map/ppermute | solution.py:237
  21.7 21.2 %collective-permute-done.3 = f32[16]{0:T(128)S(1)} collective-permute-done((f32[16]{0:T(128)S(1)}, f32[16]{0:T(128)S(1)}, u32[]{:S(2)}, u32[]{:S(2)}) %collective-permute-start.3) | collective-permute-done | bytes 96 | tf_op jit(solution)/shard_map/ppermute | solution.py:237
  42.9 1.5 %select_select_fusion = f32[16,64,128]{2,1,0:T(8,128)S(1)} fusion(f32[16,64,128]{2,1,0:T(8,128)S(1)} %collective-permute-done.2, f32[16,64,128]{2,1,0:T(8,128)} %select_add_fusion, f32[16,64,128]{2,1,0:T(8,128)} %multiply_add_fusion.2, f32[16,64,128]{2,1,0:T(8,128)S(1)} %collective-permute-done.5, f32[16]{0:T(128)S(1)} %get-tuple-element.44, ...), kind=kLoop, calls=%fused_computation.11 | loop fusion | flops 1441792 | bytes 2621570 | tf_op jit(solution)/shard_map/jit(_where)/select_n | solution.py:272
  44.3 1.8 %collective-permute-start.6 = (f32[16,64,128]{2,1,0:T(8,128)S(1)}, f32[16,64,128]{2,1,0:T(8,128)S(1)}, u32[]{:S(2)}, u32[]{:S(2)}) collective-permute-start(f32[16,64,128]{2,1,0:T(8,128)S(1)} %select_select_fusion), channel_id=1, source_target_pairs={{0,16},{4,20},{8,24},{12,28},{16,0},{20,4},{24,8},{28,12},{1,17},{... | collective-permute-start | bytes 1572872 | tf_op jit(solution)/shard_map/ppermute | solution.py:237
  46.2 11.9 %collective-permute-done.6 = f32[16,64,128]{2,1,0:T(8,128)S(1)} collective-permute-done((f32[16,64,128]{2,1,0:T(8,128)S(1)}, f32[16,64,128]{2,1,0:T(8,128)S(1)}, u32[]{:S(2)}, u32[]{:S(2)}) %collective-permute-start.6) | collective-permute-done | bytes 524320 | tf_op jit(solution)/shard_map/ppermute | solution.py:237
  58.0 0.8 copy-done
  58.8 1.3 %fusion.1 = (f32[16,64,128]{2,1,0:T(8,128)}, f32[16,64,128]{2,1,0:T(8,128)}) fusion(f32[16]{0:T(128)S(1)} %exp.22, pred[]{:T(512)S(6)} %eq.20, f32[16,64,128]{2,1,0:T(8,128)S(1)} %bitcast.31, f32[16,64,128]{2,1,0:T(8,128)S(1)} %collective-permute-done.4, f32[16,64,128]{2,1,0:T(8,128)S(1)} %collective-permute-done.6, f32[16]{0:T(128)S(1)} %get-tuple-element.67, ...), kind=kLoop, calls=%fused_computation.7 | loop fusion | flops 2097152 | bytes 4718851 | tf_op jit(solution)/shard_map/jit(_where)/select_n | solution.py:288
  60.7 16.5 %within.1 = (f32[2048,512]{1,0:T(8,128)}, f32[32,512]{1,0:T(8,128)}, f32[32,512]{1,0:T(8,128)}, f32[4,128,128]{2,1,0:T(8,128)}) custom-call(bf16[512,2048]{1,0:T(8,128)(2,1)} %x_ref.5, bf16[2048,512]{1,0:T(8,128)(2,1)} %get-tuple-element.22.xt_ref, bf16[2048,512]{1,0:T(8,128)(2,1)} %get-tuple-element.23.gt_ref, f32[32,512]{1,0:T(8,128)} %get-tuple-element.24.dt_ref, ...), custom_call_target="tpu_custom_call" | custom-call | flops 3221225472 | bytes 14680064 | tf_op jit(solution)/shard_map/within/pallas_call | solution.py:361
  77.7 1.4 %broadcast_select_fusion = (f32[16,64,128]{2,1,0:T(8,128)S(1)}, f32[16,64,128]{2,1,0:T(8,128)S(1)}) fusion(f32[16,64,128]{2,1,0:T(8,128)S(1)} %get-tuple-element.41, f32[16,64,128]{2,1,0:T(8,128)} %collective-permute-done.8, pred[]{:T(512)S(6)} %eq.20, f32[16,64,128]{2,1,0:T(8,128)S(1)} %get-tuple-element.64, f32[16,64,128]{2,1,0:T(8,128)} %collective-permute-done.7), kind=kLoop, calls=%fused_computation.20 | loop fusion | flops 262144 | bytes 3145729 | tf_op jit(solution)/shard_map/jit(_where)/select_n | solution.py:292
  79.0 1.1 pad_maximum_fusion.1
  80.1 1.1 pad_maximum_fusion
  81.2 15.5 %across.1 = (bf16[512,2048]{1,0:T(8,128)(2,1)}, f32[32,512]{1,0:T(8,128)}, f32[32,128]{1,0:T(8,128)}, f32[2,512,128]{2,1,0:T(8,128)}) custom-call(bf16[512,2048]{1,0:T(8,128)(2,1)} %x_ref.5, bf16[512,2048]{1,0:T(8,128)(2,1)} %g_ref.3, bf16[2048,512]{1,0:T(8,128)(2,1)} %get-tuple-element.22.xt_ref, bf16[2048,512]{1,0:T(8,128)(2,1)} %get-tuple-element.23.gt_ref, ...), custom_call_target="tpu_custom_call" | custom-call | tf_op jit(solution)/shard_map/across/pallas_call | solution.py:378
  96.7 1.1 constant_dynamic-slice_fusion.2
  97.8 2.6 %collective-permute-start.10 = (f32[2,128,128]{2,1,0:T(8,128)S(1)}, f32[2,128,128]{2,1,0:T(8,128)S(1)}, u32[]{:S(2)}, u32[]{:S(2)}) collective-permute-start(f32[2,128,128]{2,1,0:T(8,128)S(1)} %get-tuple-element.62), channel_id=1, source_target_pairs={{0,2},{1,3},{2,0},{3,1},{4,6},{5,7},{6,4},{7,5},{8,10},{9,11},{10,... | collective-permute-start | bytes 393224 | tf_op jit(solution)/shard_map/ppermute | solution.py:302
  100.4 1.3 %collective-permute-start.11 = (f32[2,128,128]{2,1,0:T(8,128)S(1)}, f32[2,128,128]{2,1,0:T(8,128)S(1)}, u32[]{:S(2)}, u32[]{:S(2)}) collective-permute-start(f32[2,128,128]{2,1,0:T(8,128)S(1)} %get-tuple-element.61), channel_id=1, source_target_pairs={{0,3},{1,0},{2,1},{3,2},{4,7},{5,4},{6,5},{7,6},{8,11},{9,8},{10,9... | collective-permute-start | bytes 393224 | tf_op jit(solution)/shard_map/ppermute | solution.py:302
  102.4 6.4 %collective-permute-done.10 = f32[2,128,128]{2,1,0:T(8,128)S(1)} collective-permute-done((f32[2,128,128]{2,1,0:T(8,128)S(1)}, f32[2,128,128]{2,1,0:T(8,128)S(1)}, u32[]{:S(2)}, u32[]{:S(2)}) %collective-permute-start.10) | collective-permute-done | bytes 131104 | tf_op jit(solution)/shard_map/ppermute | solution.py:302
  108.8 2.1 %collective-permute-done.9 = f32[2,128,128]{2,1,0:T(8,128)S(1)} collective-permute-done((f32[2,128,128]{2,1,0:T(8,128)S(1)}, f32[2,128,128]{2,1,0:T(8,128)S(1)}, u32[]{:S(2)}, u32[]{:S(2)}) %collective-permute-start.9) | collective-permute-done | bytes 131104 | tf_op jit(solution)/shard_map/ppermute | solution.py:302
  110.9 0.9 add_add_fusion
  111.8 2.4 %collective-permute-start.12 = (f32[2,128,128]{2,1,0:T(8,128)S(1)}, f32[2,128,128]{2,1,0:T(8,128)S(1)}, u32[]{:S(2)}, u32[]{:S(2)}) collective-permute-start(f32[2,128,128]{2,1,0:T(8,128)S(1)} %add_add_fusion), channel_id=1, source_target_pairs={{0,1},{1,2},{2,3},{3,0},{4,5},{5,6},{6,7},{7,4},{8,9},{9,10},{10,1... | collective-permute-start | bytes 393224 | tf_op jit(solution)/shard_map/ppermute | solution.py:302
  114.2 2.0 %collective-permute-start.13 = (f32[2,128,128]{2,1,0:T(8,128)S(1)}, f32[2,128,128]{2,1,0:T(8,128)S(1)}, u32[]{:S(2)}, u32[]{:S(2)}) collective-permute-start(f32[2,128,128]{2,1,0:T(8,128)S(1)} %add_add_fusion), channel_id=1, source_target_pairs={{0,2},{1,3},{2,0},{3,1},{4,6},{5,7},{6,4},{7,5},{8,10},{9,11},{10,... | collective-permute-start | bytes 393224 | tf_op jit(solution)/shard_map/ppermute | solution.py:302
  116.2 2.8 %collective-permute-start.14 = (f32[2,128,128]{2,1,0:T(8,128)S(1)}, f32[2,128,128]{2,1,0:T(8,128)S(1)}, u32[]{:S(2)}, u32[]{:S(2)}) collective-permute-start(f32[2,128,128]{2,1,0:T(8,128)S(1)} %add_add_fusion), channel_id=1, source_target_pairs={{0,3},{1,0},{2,1},{3,2},{4,7},{5,4},{6,5},{7,6},{8,11},{9,8},{10,9... | collective-permute-start | bytes 393224 | tf_op jit(solution)/shard_map/ppermute | solution.py:302
  119.8 1.5 %collective-permute-start.16 = (f32[32,3]{1,0:T(8,128)S(1)}, f32[32,3]{1,0:T(8,128)S(1)}, u32[]{:S(2)}, u32[]{:S(2)}) collective-permute-start(f32[32,3]{1,0:T(8,128)S(1)} %slice_add_fusion), channel_id=1, source_target_pairs={{0,8},{4,12},{8,0},{12,4},{16,24},{20,28},{24,16},{28,20},{1,9},{5... | collective-permute-start | bytes 1160 | tf_op jit(solution)/shard_map/ppermute | solution.py:237
  121.3 2.2 %collective-permute-done.16 = f32[32,3]{1,0:T(8,128)S(1)} collective-permute-done((f32[32,3]{1,0:T(8,128)S(1)}, f32[32,3]{1,0:T(8,128)S(1)}, u32[]{:S(2)}, u32[]{:S(2)}) %collective-permute-start.16) | collective-permute-done | bytes 416 | tf_op jit(solution)/shard_map/ppermute | solution.py:237
  123.5 1.5 %collective-permute-start.17 = (f32[32,3]{1,0:T(8,128)S(1)}, f32[32,3]{1,0:T(8,128)S(1)}, u32[]{:S(2)}, u32[]{:S(2)}) collective-permute-start(f32[32,3]{1,0:T(8,128)S(1)} %add.156), channel_id=1, source_target_pairs={{0,16},{4,20},{8,24},{12,28},{16,0},{20,4},{24,8},{28,12},{1,17},{... | collective-permute-start | bytes 1160 | tf_op jit(solution)/shard_map/ppermute | solution.py:237
  125.1 2.2 %collective-permute-done.17 = f32[32,3]{1,0:T(8,128)S(1)} collective-permute-done((f32[32,3]{1,0:T(8,128)S(1)}, f32[32,3]{1,0:T(8,128)S(1)}, u32[]{:S(2)}, u32[]{:S(2)}) %collective-permute-start.17) | collective-permute-done | bytes 416 | tf_op jit(solution)/shard_map/ppermute | solution.py:237
  (41 shorter events, 8.1 us)
Async XLA Ops:
  10.4 4.6 %copy-start.2 = (f32[32,128]{1,0:T(8,128)S(1)}, f32[32,128]{1,0:T(8,128)}, u32[]{:S(2)}) copy-start(f32[32,128]{1,0:T(8,128)} %get-tuple-element.28) | copy-start | bytes 49156
  11.3 3.9 %collective-permute-start = (f32[32]{0:T(128)S(1)}, f32[32]{0:T(128)S(1)}, u32[]{:S(2)}, u32[]{:S(2)}) collective-permute-start(f32[32]{0:T(128)S(1)} %slice_reduce_fusion.3), channel_id=1, source_target_pairs={{0,4},{4,0},{8,12},{12,8},{16,20},{20,16},{24,28},{28,24},{1,5},{5... | collective-permute-start | bytes 392 | tf_op jit(solution)/shard_map/ppermute | solution.py:237
  13.1 2.1 %collective-permute-start.4 = (f32[16,64,128]{2,1,0:T(8,128)S(1)}, f32[16,64,128]{2,1,0:T(8,128)S(1)}, u32[]{:S(2)}, u32[]{:S(2)}) collective-permute-start(f32[16,64,128]{2,1,0:T(8,128)S(1)} %bitcast.39), channel_id=1, source_target_pairs={{0,4},{4,0},{8,12},{12,8},{16,20},{20,16},{24,28},{28,24},{1,5},{5... | collective-permute-start | bytes 1572872 | tf_op jit(solution)/shard_map/ppermute | solution.py:237
  14.5 4.2 %collective-permute-start.1 = (f32[16,64,128]{2,1,0:T(8,128)S(1)}, f32[16,64,128]{2,1,0:T(8,128)S(1)}, u32[]{:S(2)}, u32[]{:S(2)}) collective-permute-start(f32[16,64,128]{2,1,0:T(8,128)S(1)} %bitcast.38), channel_id=1, source_target_pairs={{0,4},{4,0},{8,12},{12,8},{16,20},{20,16},{24,28},{28,24},{1,5},{5... | collective-permute-start | bytes 1572872 | tf_op jit(solution)/shard_map/ppermute | solution.py:237
  16.2 26.6 %collective-permute-start.5 = (f32[16,64,128]{2,1,0:T(8,128)}, f32[16,64,128]{2,1,0:T(8,128)S(1)}, u32[]{:S(2)}, u32[]{:S(2)}) collective-permute-start(f32[16,64,128]{2,1,0:T(8,128)} %multiply_add_fusion.2), channel_id=1, source_target_pairs={{0,8},{4,12},{8,0},{12,4},{16,24},{20,28},{24,16},{28,20},{1,9},{5... | collective-permute-start | bytes 1572872 | tf_op jit(solution)/shard_map/ppermute | solution.py:237
  19.6 23.2 %collective-permute-start.2 = (f32[16,64,128]{2,1,0:T(8,128)}, f32[16,64,128]{2,1,0:T(8,128)S(1)}, u32[]{:S(2)}, u32[]{:S(2)}) collective-permute-start(f32[16,64,128]{2,1,0:T(8,128)} %select_add_fusion), channel_id=1, source_target_pairs={{0,8},{4,12},{8,0},{12,4},{16,24},{20,28},{24,16},{28,20},{1,9},{5... | collective-permute-start | bytes 1572872 | tf_op jit(solution)/shard_map/ppermute | solution.py:237
  20.3 22.5 %collective-permute-start.3 = (f32[16]{0:T(128)S(1)}, f32[16]{0:T(128)S(1)}, u32[]{:S(2)}, u32[]{:S(2)}) collective-permute-start(f32[16]{0:T(128)S(1)} %get-tuple-element.45), channel_id=1, source_target_pairs={{0,8},{4,12},{8,0},{12,4},{16,24},{20,28},{24,16},{28,20},{1,9},{5... | collective-permute-start | bytes 200 | tf_op jit(solution)/shard_map/ppermute | solution.py:237
  44.3 13.7 %collective-permute-start.6 = (f32[16,64,128]{2,1,0:T(8,128)S(1)}, f32[16,64,128]{2,1,0:T(8,128)S(1)}, u32[]{:S(2)}, u32[]{:S(2)}) collective-permute-start(f32[16,64,128]{2,1,0:T(8,128)S(1)} %select_select_fusion), channel_id=1, source_target_pairs={{0,16},{4,20},{8,24},{12,28},{16,0},{20,4},{24,8},{28,12},{1,17},{... | collective-permute-start | bytes 1572872 | tf_op jit(solution)/shard_map/ppermute | solution.py:237
  58.0 0.8 copy-start
  60.2 17.0 %collective-permute-start.7 = (f32[16,64,128]{2,1,0:T(8,128)}, f32[16,64,128]{2,1,0:T(8,128)}, u32[]{:S(2)}, u32[]{:S(2)}) collective-permute-start(f32[16,64,128]{2,1,0:T(8,128)} %get-tuple-element.66), channel_id=1, source_target_pairs={{0,4},{4,0},{8,12},{12,8},{16,20},{20,16},{24,28},{28,24},{1,5},{5... | collective-permute-start | bytes 1572872 | tf_op jit(solution)/shard_map/ppermute | solution.py:237
  60.2 17.0 %collective-permute-start.8 = (f32[16,64,128]{2,1,0:T(8,128)}, f32[16,64,128]{2,1,0:T(8,128)}, u32[]{:S(2)}, u32[]{:S(2)}) collective-permute-start(f32[16,64,128]{2,1,0:T(8,128)} %get-tuple-element.65), channel_id=1, source_target_pairs={{0,4},{4,0},{8,12},{12,8},{16,20},{20,16},{24,28},{28,24},{1,5},{5... | collective-permute-start | bytes 1572872 | tf_op jit(solution)/shard_map/ppermute | solution.py:237
  60.7 16.5 %copy-start.1 = (f32[16,64,128]{2,1,0:T(8,128)S(1)}, f32[16,64,128]{2,1,0:T(8,128)}, u32[]{:S(2)}) copy-start(f32[16,64,128]{2,1,0:T(8,128)} %copy-done) | copy-start | bytes 1572868
  97.8 11.0 %collective-permute-start.10 = (f32[2,128,128]{2,1,0:T(8,128)S(1)}, f32[2,128,128]{2,1,0:T(8,128)S(1)}, u32[]{:S(2)}, u32[]{:S(2)}) collective-permute-start(f32[2,128,128]{2,1,0:T(8,128)S(1)} %get-tuple-element.62), channel_id=1, source_target_pairs={{0,2},{1,3},{2,0},{3,1},{4,6},{5,7},{6,4},{7,5},{8,10},{9,11},{10,... | collective-permute-start | bytes 393224 | tf_op jit(solution)/shard_map/ppermute | solution.py:302
  100.4 8.4 %collective-permute-start.11 = (f32[2,128,128]{2,1,0:T(8,128)S(1)}, f32[2,128,128]{2,1,0:T(8,128)S(1)}, u32[]{:S(2)}, u32[]{:S(2)}) collective-permute-start(f32[2,128,128]{2,1,0:T(8,128)S(1)} %get-tuple-element.61), channel_id=1, source_target_pairs={{0,3},{1,0},{2,1},{3,2},{4,7},{5,4},{6,5},{7,6},{8,11},{9,8},{10,9... | collective-permute-start | bytes 393224 | tf_op jit(solution)/shard_map/ppermute | solution.py:302
  101.7 9.1 %collective-permute-start.9 = (f32[2,128,128]{2,1,0:T(8,128)S(1)}, f32[2,128,128]{2,1,0:T(8,128)S(1)}, u32[]{:S(2)}, u32[]{:S(2)}) collective-permute-start(f32[2,128,128]{2,1,0:T(8,128)S(1)} %get-tuple-element.60), channel_id=1, source_target_pairs={{0,1},{1,2},{2,3},{3,0},{4,5},{5,6},{6,7},{7,4},{8,9},{9,10},{10,1... | collective-permute-start | bytes 393224 | tf_op jit(solution)/shard_map/ppermute | solution.py:302
  102.4 16.6 %collective-permute-start.15 = (f32[32,3]{1,0:T(8,128)}, f32[32,3]{1,0:T(8,128)S(1)}, u32[]{:S(2)}, u32[]{:S(2)}) collective-permute-start(f32[32,3]{1,0:T(8,128)} %bitcast.44), channel_id=1, source_target_pairs={{0,4},{4,0},{8,12},{12,8},{16,20},{20,16},{24,28},{28,24},{1,5},{5... | collective-permute-start | bytes 1160 | tf_op jit(solution)/shard_map/ppermute | solution.py:237
  111.8 16.2 %collective-permute-start.12 = (f32[2,128,128]{2,1,0:T(8,128)S(1)}, f32[2,128,128]{2,1,0:T(8,128)S(1)}, u32[]{:S(2)}, u32[]{:S(2)}) collective-permute-start(f32[2,128,128]{2,1,0:T(8,128)S(1)} %add_add_fusion), channel_id=1, source_target_pairs={{0,1},{1,2},{2,3},{3,0},{4,5},{5,6},{6,7},{7,4},{8,9},{9,10},{10,1... | collective-permute-start | bytes 393224 | tf_op jit(solution)/shard_map/ppermute | solution.py:302
  114.2 13.8 %collective-permute-start.13 = (f32[2,128,128]{2,1,0:T(8,128)S(1)}, f32[2,128,128]{2,1,0:T(8,128)S(1)}, u32[]{:S(2)}, u32[]{:S(2)}) collective-permute-start(f32[2,128,128]{2,1,0:T(8,128)S(1)} %add_add_fusion), channel_id=1, source_target_pairs={{0,2},{1,3},{2,0},{3,1},{4,6},{5,7},{6,4},{7,5},{8,10},{9,11},{10,... | collective-permute-start | bytes 393224 | tf_op jit(solution)/shard_map/ppermute | solution.py:302
  116.2 11.8 %collective-permute-start.14 = (f32[2,128,128]{2,1,0:T(8,128)S(1)}, f32[2,128,128]{2,1,0:T(8,128)S(1)}, u32[]{:S(2)}, u32[]{:S(2)}) collective-permute-start(f32[2,128,128]{2,1,0:T(8,128)S(1)} %add_add_fusion), channel_id=1, source_target_pairs={{0,3},{1,0},{2,1},{3,2},{4,7},{5,4},{6,5},{7,6},{8,11},{9,8},{10,9... | collective-permute-start | bytes 393224 | tf_op jit(solution)/shard_map/ppermute | solution.py:302
  119.8 3.7 %collective-permute-start.16 = (f32[32,3]{1,0:T(8,128)S(1)}, f32[32,3]{1,0:T(8,128)S(1)}, u32[]{:S(2)}, u32[]{:S(2)}) collective-permute-start(f32[32,3]{1,0:T(8,128)S(1)} %slice_add_fusion), channel_id=1, source_target_pairs={{0,8},{4,12},{8,0},{12,4},{16,24},{20,28},{24,16},{28,20},{1,9},{5... | collective-permute-start | bytes 1160 | tf_op jit(solution)/shard_map/ppermute | solution.py:237
  123.5 3.7 %collective-permute-start.17 = (f32[32,3]{1,0:T(8,128)S(1)}, f32[32,3]{1,0:T(8,128)S(1)}, u32[]{:S(2)}, u32[]{:S(2)}) collective-permute-start(f32[32,3]{1,0:T(8,128)S(1)} %add.156), channel_id=1, source_target_pairs={{0,16},{4,20},{8,24},{12,28},{16,0},{20,4},{24,8},{28,12},{1,17},{... | collective-permute-start | bytes 1160 | tf_op jit(solution)/shard_map/ppermute | solution.py:237

commit v2 on v1

--- a/solution.py
+++ b/solution.py
@@ -63,9 +63,10 @@
     return slice(c * CHUNK, (c + 1) * CHUNK)
 
 
-def states_kernel(x_ref, g_ref, raw_ref, knob_ref, b_ref, c_ref,
-                  xt_ref, gt_ref, dt_ref, cum_ref, end_ref, s_ref, r_ref):
-    _, tokens = raw_ref.shape
+def states_kernel(odd_ref, x_ref, g_ref, raw_ref, knob_ref, b_ref, c_ref,
+                  xt_ref, gt_ref, dt_ref, cum_ref, end_ref, s_ref, r_ref,
+                  s_mine_ref, s_theirs_ref, r_mine_ref, r_theirs_ref):
+    heads, tokens = raw_ref.shape
     chunks = tokens // CHUNK
     dt = softplus(raw_ref[...] + knob_ref[:, 0:1])
     dt_ref[...] = dt
@@ -95,6 +96,20 @@
         added = mm(high, cc) + mm(low, cc)
         back = added if back is None else per_head(jnp.exp(ends[c]), back) + added
         r_ref[c] = back
+    for value, mine, theirs in ((state, s_mine_ref, s_theirs_ref), (back, r_mine_ref, r_theirs_ref)):
+        shaped = value.reshape(heads, value.shape[0] // heads, value.shape[1])
+        half = shaped.shape[1] // 2
+        first, second = shaped[:, :half], shaped[:, half:]
+
+        @pl.when(odd_ref[0] == 0)
+        def _():
+            mine[...] = first
+            theirs[...] = second
+
+        @pl.when(odd_ref[0] == 1)
+        def _():
+            mine[...] = second
+            theirs[...] = first
 
 
 def within_kernel(x_ref, xt_ref, gt_ref, dt_ref, cum_ref, b_ref, c_ref,
@@ -140,10 +155,11 @@
     lax.fori_loop(0, tokens // CHUNK, one_chunk, 0)
 
 
-def across_kernel(x_ref, g_ref, xt_ref, gt_ref, raw_ref, knob_ref, dt_ref, cum_ref,
-                  s_ref, r_ref, sin_ref, rin_ref, dxt_ref, row_ref, col_ref,
+def across_kernel(odd_ref, x_ref, g_ref, xt_ref, gt_ref, raw_ref, knob_ref, dt_ref, cum_ref,
+                  s_ref, r_ref, s_keep_ref, s_back_ref, r_keep_ref, r_back_ref,
+                  dxt_ref, row_ref, col_ref,
                   b_ref, c_ref, dg_ref,
-                  gx_ref, graw_ref, gparam_ref, dbc_ref):
+                  gx_ref, graw_ref, gparam_ref, dbc_ref, in_ref):
     db_ref, dc_ref = dbc_ref.at[0], dbc_ref.at[1]
     heads, tokens = dt_ref.shape
     chunks = tokens // CHUNK
@@ -158,6 +174,21 @@
             high, low = split(dg_ref[c].T)
             dc_ref[span_of(c), :] = mm(high, b_ref[span_of(c), :]) + mm(low, b_ref[span_of(c), :])
 
+    half = size // 2
+    for k, (keep, given) in enumerate(((s_keep_ref, s_back_ref), (r_keep_ref, r_back_ref))):
+
+        @pl.when(odd_ref[0] == 0)
+        def _():
+            in_ref[k, :, :half, :] = keep[...]
+            in_ref[k, :, half:, :] = given[...]
+
+        @pl.when(odd_ref[0] == 1)
+        def _():
+            in_ref[k, :, :half, :] = given[...]
+            in_ref[k, :, half:, :] = keep[...]
+
+    s_in = in_ref[0].reshape(xt_ref.shape[0], b_ref.shape[1])
+    r_in = in_ref[1].reshape(xt_ref.shape[0], b_ref.shape[1])
     ends = [lanes(cum_ref[:, (c + 1) * CHUNK - 1:(c + 1) * CHUNK]) for c in range(chunks)]
     before = [jnp.zeros_like(ends[0])]
     for end in ends:
@@ -173,10 +204,10 @@
         cum, dt = cum_ref[:, at], dt_ref[:, at]
         reach = jnp.exp(cum)
         weight = jnp.exp(ends[c] - cum) * dt
-        state = per_head(jnp.exp(before[c]), sin_ref[...])
+        state = per_head(jnp.exp(before[c]), s_in)
         if c > 0:
             state = state + s_ref[c - 1]
-        back = per_head(jnp.exp(after[c + 1]), rin_ref[...])
+        back = per_head(jnp.exp(after[c + 1]), r_in)
         if c < chunks - 1:
             back = back + r_ref[c + 1]
         s_high, s_low = split(state)
@@ -210,8 +241,8 @@
                 db = db + xr[:, j * width:(j + 1) * width] * weight_t[:, h:h + 1]
         dc_ref[at, :] += dc
         db_ref[at, :] += db
-    last = s_ref[chunks - 1] + per_head(jnp.exp(before[chunks]), sin_ref[...])
-    beyond = lanes(jnp.sum(head_sums(last * rin_ref[...], heads), axis=1, keepdims=True))
+    last = s_ref[chunks - 1] + per_head(jnp.exp(before[chunks]), s_in)
+    beyond = lanes(jnp.sum(head_sums(last * r_in, heads), axis=1, keepdims=True))
     suffix = triangle(True).astype(F32)
     g_rate = jnp.zeros((heads, 1), F32)
     g_bias = jnp.zeros((heads, 1), F32)
@@ -239,23 +270,15 @@
 
 def carried(span, states, adjoints, axis):
     peers, place = lax.axis_size(axis), lax.axis_index(axis)
-    heads = span.shape[0]
-    half = heads // 2
     odd = (place % 2) == 1
-
-    def halves(whole):
-        first, second = whole[:half], whole[half:]
-        return jnp.where(odd, second, first), jnp.where(odd, first, second)
+    (s_mine, s_theirs), (r_mine, r_theirs) = states, adjoints
 
     def scale(log):
         return jnp.exp(log)[:, None, None]
 
-    s_mine, s_theirs = halves(states)
-    r_mine, r_theirs = halves(adjoints)
     other = hypercube_shift(span, axis, 1)
     s_got, r_got = hypercube_shift((s_theirs, r_theirs), axis, 1)
-    log_mine, log_got = halves(span)[0], halves(other)[0]
-    log_even, log_odd = jnp.where(odd, log_got, log_mine), jnp.where(odd, log_mine, log_got)
+    log_even, log_odd = jnp.where(odd, other, span), jnp.where(odd, span, other)
     s_even, s_odd = jnp.where(odd, s_got, s_mine), jnp.where(odd, s_mine, s_got)
     r_even, r_odd = jnp.where(odd, r_got, r_mine), jnp.where(odd, r_mine, r_got)
     s_all = scale(log_odd) * s_even + s_odd
@@ -287,11 +310,7 @@
     s_keep, s_give = jnp.where(odd, s_for_odd, s_pre), jnp.where(odd, s_pre, s_for_odd)
     r_keep, r_give = jnp.where(odd, r_pre, r_for_even), jnp.where(odd, r_for_even, r_pre)
     s_back, r_back = hypercube_shift((s_give, r_give), axis, 1)
-
-    def whole(keep, back):
-        return jnp.concatenate([jnp.where(odd, back, keep), jnp.where(odd, keep, back)], axis=0)
-
-    return whole(s_keep, s_back), whole(r_keep, r_back)
+    return s_keep, s_back, r_keep, r_back
 
 
 def reduce_over(value, axis):
@@ -304,11 +323,16 @@
     def piece_of(owner):
         return lax.dynamic_slice_in_dim(value, owner * rows, rows, axis=1)
 
-    got = [shift(piece_of((place + step) % peers), step) for step in range(1, peers)]
+    got = []
+    for step in range(1, peers):
+        got.append(shift(piece_of((place + step) % peers), step))
     total = piece_of(place)
     for piece in got:
         total = total + piece
-    every = jnp.stack([total] + [shift(total, step) for step in range(1, peers)])
+    every = [total]
+    for step in range(1, peers):
+        every.append(shift(total, step))
+    every = jnp.stack(every)
     ordered = [every[(place - owner) % peers] for owner in range(peers)]
     return [jnp.concatenate([piece[k] for piece in ordered], axis=0) for k in range(2)]
 
@@ -331,32 +355,30 @@
     head_lanes = pl.BlockSpec((GROUP, CHUNK), lambda i: (i, 0))
     head_knobs = pl.BlockSpec((GROUP, 3), lambda i: (i, 0))
     projection = pl.BlockSpec((tokens, state), lambda i: (0, 0))
-    state_block = pl.BlockSpec((wide, state), lambda i: (i, 0))
+    half_block = pl.BlockSpec((GROUP, size // 2, state), lambda i: (i, 0, 0))
+    half_shape = shape(heads, size // 2, state)
+    scalar = pl.BlockSpec(memory_space=pltpu.SMEM)
+    odd = (lax.axis_index("ctx") % 2).astype(jnp.int32).reshape(1)
     state_blocks = pl.BlockSpec((chunks, wide, state), lambda i: (0, i, 0))
     projections = pl.BlockSpec((2, tokens, state), lambda i: (0, 0, 0))
     score_blocks = pl.BlockSpec((chunks, CHUNK, CHUNK), lambda i: (0, 0, 0))
     knobs = jnp.stack([step_bias, decay_rate, skip_gain], axis=1)
 
-    xt, gt, dt, cum, end, s_loc, r_loc = pl.pallas_call(
+    xt, gt, dt, cum, end, s_loc, r_loc, *halves = pl.pallas_call(
         states_kernel,
         grid=grid,
-        in_specs=[tokens_by_wide, tokens_by_wide, head_rows, head_knobs,
+        in_specs=[scalar, tokens_by_wide, tokens_by_wide, head_rows, head_knobs,
                   projection, projection],
         out_specs=[wide_by_tokens, wide_by_tokens, head_rows, head_rows, head_lanes,
-                   state_blocks, state_blocks],
+                   state_blocks, state_blocks] + [half_block] * 4,
         out_shape=[shape(width, tokens, dtype=BF16), shape(width, tokens, dtype=BF16),
                    shape(heads, tokens), shape(heads, tokens), shape(heads, CHUNK),
-                   shape(chunks, width, state), shape(chunks, width, state)],
+                   shape(chunks, width, state), shape(chunks, width, state)] + [half_shape] * 4,
         compiler_params=PARAMS,
         name="states",
-    )(tokens_x, grad_y, raw_dt, knobs, in_b, in_c)
-
-    s_in, r_in = carried(
-        end[:, 0],
-        s_loc[chunks - 1].reshape(heads, size, state),
-        r_loc[0].reshape(heads, size, state),
-        "ctx",
-    )
+    )(odd, tokens_x, grad_y, raw_dt, knobs, in_b, in_c)
+
+    arrived = carried(end[:, 0], halves[:2], halves[2:], "ctx")
 
     dxt, row, col, dg = pl.pallas_call(
         within_kernel,
@@ -378,17 +400,18 @@
     grad_x, grad_raw, params, grad_bc = pl.pallas_call(
         across_kernel,
         grid=grid,
-        in_specs=[tokens_by_wide, tokens_by_wide, wide_by_tokens, wide_by_tokens, head_rows,
+        in_specs=[scalar, tokens_by_wide, tokens_by_wide, wide_by_tokens, wide_by_tokens, head_rows,
                   head_knobs, head_rows, head_rows, state_blocks,
-                  state_blocks, state_block, state_block, wide_by_tokens, head_rows, head_rows,
+                  state_blocks, half_block, half_block, half_block, half_block, wide_by_tokens, head_rows, head_rows,
                   projection, projection, score_blocks],
         out_specs=[tokens_by_wide, head_rows, head_lanes, projections],
         out_shape=[shape(tokens, width, dtype=BF16), shape(heads, tokens), shape(heads, CHUNK),
                    shape(2, tokens, state)],
+        scratch_shapes=[pltpu.VMEM((2, GROUP, size, state), F32)],
         compiler_params=PARAMS,
         name="across",
-    )(tokens_x, grad_y, xt, gt, raw_dt, knobs, dt, cum, s_loc, r_loc,
-      s_in.reshape(width, state), r_in.reshape(width, state), dxt, row, col, in_b, in_c, dg)
+    )(odd, tokens_x, grad_y, xt, gt, raw_dt, knobs, dt, cum, s_loc, r_loc,
+      *arrived, dxt, row, col, in_b, in_c, dg)
 
     grad_b, grad_c = reduce_over(grad_bc, "head")
     params = params[:, :3]

time: 130 us -> 126 us (0.969)
  other arithmetic: 15.2 us -> 10.4 us
  starting transfers between devices: 23 us -> 20.6 us
  waiting for transfers between devices: 46 us -> 47.6 us
    select_n x5 -> x0, other arithmetic: 4.43 us -> none  [the longest x3 2.65 us: halves(): return (jnp.where(odd, second, first), jnp.where(odd, first, second))]
    ppermute x6, starting transfers between devices: 11.9 us -> 9.28 us  [shift(): lax.ppermute(piece, axis, [(i, (i + step) % peers) for i in range(peers)])]
    ppermute x6, waiting for transfers between devices: 8.47 us -> 10.9 us  [shift(): lax.ppermute(piece, axis, [(i, (i + step) % peers) for i in range(peers)])]
    concatenate x2 -> x0, other arithmetic: 2.13 us -> none  [whole(): jnp.concatenate([jnp.where(odd, back, keep), jnp.where(odd, keep, back)],...]
  transfers between devices with their start and end apart: 18 -> 18, of which waited for: 6 -> 8; matrix products, arithmetic and copies ran while one was open for 5% -> 6% of each run, Pallas kernels for 13% -> 13%
where the time goes in v2:
time: 126 us; the launch traced here: 125 us
  waiting for transfers between devices  47.6 us (38%)
  Pallas kernels  41.6 us (33%)
  starting transfers between devices  20.6 us (16%)
  other arithmetic  10.4 us (8%)
  local copies, waits for them, and re-layouts  4.32 us (3%)
    ppermute x12, waiting for transfers between devices, hypercube_shift(): return lax.ppermute(value, axis, [(i, i ^ distance) for i in range(peers)])  36.8 us
    pallas_call x1, Pallas kernels, on_device(): pl.pallas_call(within_kernel, grid=grid, in_specs=[tokens_by_wide, wide_b...  16.5 us
    pallas_call x1, Pallas kernels, on_device(): pl.pallas_call(across_kernel, grid=grid, in_specs=[scalar, tokens_by_wide...  15.7 us
    ppermute x12, starting transfers between devices, hypercube_shift(): return lax.ppermute(value, axis, [(i, i ^ distance) for i in range(peers)])  11.4 us
    ppermute x6, waiting for transfers between devices, shift(): lax.ppermute(piece, axis, [(i, (i + step) % peers) for i in range(peers)])  10.9 us
    pallas_call x1, Pallas kernels, on_device(): pl.pallas_call(states_kernel, grid=grid, in_specs=[scalar, tokens_by_wide...  9.37 us
    ppermute x6, starting transfers between devices, shift(): lax.ppermute(piece, axis, [(i, (i + step) % peers) for i in range(peers)])  9.28 us
  transfers between devices with their start and end apart: 18, of which 8 were waited for; matrix products, arithmetic and copies ran while one was open for 6% of the time, Pallas kernels for 13%

profile of v2, /device:TPU:0, one launch (start us, length us, event | category | flops | bytes accessed | tf_op | source)
XLA Modules:
  0.0 125.3 jit_solution(5325976316949686613)
XLA Ops:
  0.6 0.7 pad_maximum_fusion.3
  2.0 9.4 %states.1 = (bf16[2048,512]{1,0:T(8,128)(2,1)}, bf16[2048,512]{1,0:T(8,128)(2,1)}, f32[32,512]{1,0:T(8,128)}, f32[32,512]{1,0:T(8,128)}, f32[32,128]{1,0:T(8,128...) custom-call(s32[1]{0:T(128)} %bitcast.odd_ref, ...), custom_call_target="tpu_custom_call" | custom-call | tf_op jit(solution)/shard_map/states/pallas_call | solution.py:367
  12.0 0.8 slice_reduce_fusion.3
  13.4 1.1 collective-permute-done.1
  14.5 2.0 %select_add_fusion = f32[32,32,128]{2,1,0:T(8,128)} fusion(f32[32,32,128]{2,1,0:T(8,128)} %get-tuple-element.33, f32[32,32,128]{2,1,0:T(8,128)S(1)} %collective-permute-done, f32[32]{0:T(128)S(1)} %get-tuple-element.67, pred[]{:T(512)S(6)} %eq.21), kind=kLoop, calls=%fused_computation.11 | loop fusion | flops 524288 | bytes 1572993 | tf_op jit(solution)/shard_map/add | solution.py:284
  16.4 2.9 %collective-permute-start.2 = (f32[32,32,128]{2,1,0:T(8,128)}, f32[32,32,128]{2,1,0:T(8,128)S(1)}, u32[]{:S(2)}, u32[]{:S(2)}) collective-permute-start(f32[32,32,128]{2,1,0:T(8,128)} %select_add_fusion), channel_id=1, source_target_pairs={{0,8},{4,12},{8,0},{12,4},{16,24},{20,28},{24,16},{28,20},{1,9},{5... | collective-permute-start | bytes 1572872 | tf_op jit(solution)/shard_map/ppermute | solution.py:268
  19.3 2.1 %multiply_add_fusion.2 = f32[32,32,128]{2,1,0:T(8,128)} fusion(f32[32,32,128]{2,1,0:T(8,128)S(1)} %collective-permute-done.4, f32[32,32,128]{2,1,0:T(8,128)} %get-tuple-element.36, f32[32]{0:T(128)S(1)} %get-tuple-element.68, pred[]{:T(512)S(6)} %eq.21), kind=kLoop, calls=%fused_computation.10 | loop fusion | flops 524288 | bytes 1572993 | tf_op jit(solution)/shard_map/add | solution.py:285
  21.4 2.0 %collective-permute-start.3 = (f32[32]{0:T(128)S(1)}, f32[32]{0:T(128)S(1)}, u32[]{:S(2)}, u32[]{:S(2)}) collective-permute-start(f32[32]{0:T(128)S(1)} %get-tuple-element.49), channel_id=1, source_target_pairs={{0,8},{4,12},{8,0},{12,4},{16,24},{20,28},{24,16},{28,20},{1,9},{5... | collective-permute-start | bytes 392 | tf_op jit(solution)/shard_map/ppermute | solution.py:268
  23.4 19.6 %collective-permute-done.3 = f32[32]{0:T(128)S(1)} collective-permute-done((f32[32]{0:T(128)S(1)}, f32[32]{0:T(128)S(1)}, u32[]{:S(2)}, u32[]{:S(2)}) %collective-permute-start.3) | collective-permute-done | bytes 160 | tf_op jit(solution)/shard_map/ppermute | solution.py:268
  43.1 1.5 %select_select_fusion = f32[32,32,128]{2,1,0:T(8,128)S(1)} fusion(f32[32,32,128]{2,1,0:T(8,128)S(1)} %collective-permute-done.2, f32[32,32,128]{2,1,0:T(8,128)} %select_add_fusion, f32[32,32,128]{2,1,0:T(8,128)} %multiply_add_fusion.2, f32[32,32,128]{2,1,0:T(8,128)S(1)} %collective-permute-done.5, f32[32]{0:T(128)S(1)} %get-tuple-element.48, ...), kind=kLoop, calls=%fused_computation.9 | loop fusion | flops 1441792 | bytes 2621698 | tf_op jit(solution)/shard_map/jit(_where)/select_n | solution.py:295
  44.5 1.8 %collective-permute-start.6 = (f32[32,32,128]{2,1,0:T(8,128)S(1)}, f32[32,32,128]{2,1,0:T(8,128)S(1)}, u32[]{:S(2)}, u32[]{:S(2)}) collective-permute-start(f32[32,32,128]{2,1,0:T(8,128)S(1)} %select_select_fusion), channel_id=1, source_target_pairs={{0,16},{4,20},{8,24},{12,28},{16,0},{20,4},{24,8},{28,12},{1,17},{... | collective-permute-start | bytes 1572872 | tf_op jit(solution)/shard_map/ppermute | solution.py:268
  46.4 11.5 %collective-permute-done.6 = f32[32,32,128]{2,1,0:T(8,128)S(1)} collective-permute-done((f32[32,32,128]{2,1,0:T(8,128)S(1)}, f32[32,32,128]{2,1,0:T(8,128)S(1)}, u32[]{:S(2)}, u32[]{:S(2)}) %collective-permute-start.6) | collective-permute-done | bytes 524320 | tf_op jit(solution)/shard_map/ppermute | solution.py:268
  57.9 1.7 %fusion = (f32[32,32,128]{2,1,0:T(8,128)}, f32[32,32,128]{2,1,0:T(8,128)}, f32[32,32,128]{2,1,0:T(8,128)}, f32[32,32,128]{2,1,0:T(8,128)}) fusion(f32[32]{0:T(128)S(1)} %get-tuple-element.67, pred[]{:T(512)S(6)} %eq.21, f32[32,32,128]{2,1,0:T(8,128)S(1)} %copy-done.1, f32[32,32,128]{2,1,0:T(8,128)S(1)} %collective-permute-done.4, ...), kind=kLoop, calls=%fused_computation.4 | loop fusion | flops 2359296 | bytes 5767683 | tf_op jit(solution)/shard_map/jit(_where)/select_n | solution.py:311
  60.1 16.5 %within.1 = (f32[2048,512]{1,0:T(8,128)}, f32[32,512]{1,0:T(8,128)}, f32[32,512]{1,0:T(8,128)}, f32[4,128,128]{2,1,0:T(8,128)}) custom-call(bf16[512,2048]{1,0:T(8,128)(2,1)} %x_ref.5, bf16[2048,512]{1,0:T(8,128)(2,1)} %get-tuple-element.26.xt_ref, bf16[2048,512]{1,0:T(8,128)(2,1)} %get-tuple-element.27.gt_ref, f32[32,512]{1,0:T(8,128)} %get-tuple-element.28.dt_ref, ...), custom_call_target="tpu_custom_call" | custom-call | flops 3221225472 | bytes 14680064 | tf_op jit(solution)/shard_map/within/pallas_call | solution.py:383
  76.6 0.8 copy-done.2
  77.6 15.7 %across.1 = (bf16[512,2048]{1,0:T(8,128)(2,1)}, f32[32,512]{1,0:T(8,128)}, f32[32,128]{1,0:T(8,128)}, f32[2,512,128]{2,1,0:T(8,128)}) custom-call(s32[1]{0:T(128)} %bitcast.odd_ref, bf16[512,2048]{1,0:T(8,128)(2,1)} %x_ref.5, bf16[512,2048]{1,0:T(8,128)(2,1)} %g_ref.3, bf16[2048,512]{1,0:T(8,128)(2,1)} %get-tuple-element.26.xt_ref, ...), custom_call_target="tpu_custom_call" | custom-call | tf_op jit(solution)/shard_map/across/pallas_call | solution.py:400
  93.3 1.1 constant_dynamic-slice_fusion.2
  94.4 3.6 %collective-permute-start.11 = (f32[2,128,128]{2,1,0:T(8,128)S(1)}, f32[2,128,128]{2,1,0:T(8,128)S(1)}, u32[]{:S(2)}, u32[]{:S(2)}) collective-permute-start(f32[2,128,128]{2,1,0:T(8,128)S(1)} %get-tuple-element.63), channel_id=1, source_target_pairs={{0,3},{1,0},{2,1},{3,2},{4,7},{5,4},{6,5},{7,6},{8,11},{9,8},{10,9... | collective-permute-start | bytes 393224 | tf_op jit(solution)/shard_map/ppermute | solution.py:321
  98.0 1.0 collective-permute-start.9
  99.0 2.9 %collective-permute-done.11 = f32[2,128,128]{2,1,0:T(8,128)S(1)} collective-permute-done((f32[2,128,128]{2,1,0:T(8,128)S(1)}, f32[2,128,128]{2,1,0:T(8,128)S(1)}, u32[]{:S(2)}, u32[]{:S(2)}) %collective-permute-start.11) | collective-permute-done | bytes 131104 | tf_op jit(solution)/shard_map/ppermute | solution.py:321
  102.0 7.5 %collective-permute-done.10 = f32[2,128,128]{2,1,0:T(8,128)S(1)} collective-permute-done((f32[2,128,128]{2,1,0:T(8,128)S(1)}, f32[2,128,128]{2,1,0:T(8,128)S(1)}, u32[]{:S(2)}, u32[]{:S(2)}) %collective-permute-start.10) | collective-permute-done | bytes 131104 | tf_op jit(solution)/shard_map/ppermute | solution.py:321
  109.5 0.9 add_add_fusion
  110.4 1.5 %collective-permute-start.14 = (f32[2,128,128]{2,1,0:T(8,128)S(1)}, f32[2,128,128]{2,1,0:T(8,128)S(1)}, u32[]{:S(2)}, u32[]{:S(2)}) collective-permute-start(f32[2,128,128]{2,1,0:T(8,128)S(1)} %add_add_fusion), channel_id=1, source_target_pairs={{0,3},{1,0},{2,1},{3,2},{4,7},{5,4},{6,5},{7,6},{8,11},{9,8},{10,9... | collective-permute-start | bytes 393224 | tf_op jit(solution)/shard_map/ppermute | solution.py:321
  111.9 1.2 collective-permute-start.13
  113.1 1.9 %collective-permute-start.12 = (f32[2,128,128]{2,1,0:T(8,128)S(1)}, f32[2,128,128]{2,1,0:T(8,128)S(1)}, u32[]{:S(2)}, u32[]{:S(2)}) collective-permute-start(f32[2,128,128]{2,1,0:T(8,128)S(1)} %add_add_fusion), channel_id=1, source_target_pairs={{0,1},{1,2},{2,3},{3,0},{4,5},{5,6},{6,7},{7,4},{8,9},{9,10},{10,1... | collective-permute-start | bytes 393224 | tf_op jit(solution)/shard_map/ppermute | solution.py:321
  115.1 0.7 slice_add_fusion
  115.8 1.5 %collective-permute-start.16 = (f32[32,3]{1,0:T(8,128)S(1)}, f32[32,3]{1,0:T(8,128)S(1)}, u32[]{:S(2)}, u32[]{:S(2)}) collective-permute-start(f32[32,3]{1,0:T(8,128)S(1)} %slice_add_fusion), channel_id=1, source_target_pairs={{0,8},{4,12},{8,0},{12,4},{16,24},{20,28},{24,16},{28,20},{1,9},{5... | collective-permute-start | bytes 1160 | tf_op jit(solution)/shard_map/ppermute | solution.py:268
  117.3 2.2 %collective-permute-done.16 = f32[32,3]{1,0:T(8,128)S(1)} collective-permute-done((f32[32,3]{1,0:T(8,128)S(1)}, f32[32,3]{1,0:T(8,128)S(1)}, u32[]{:S(2)}, u32[]{:S(2)}) %collective-permute-start.16) | collective-permute-done | bytes 416 | tf_op jit(solution)/shard_map/ppermute | solution.py:268
  119.5 1.5 %collective-permute-start.17 = (f32[32,3]{1,0:T(8,128)S(1)}, f32[32,3]{1,0:T(8,128)S(1)}, u32[]{:S(2)}, u32[]{:S(2)}) collective-permute-start(f32[32,3]{1,0:T(8,128)S(1)} %add.157), channel_id=1, source_target_pairs={{0,16},{4,20},{8,24},{12,28},{16,0},{20,4},{24,8},{28,12},{1,17},{... | collective-permute-start | bytes 1160 | tf_op jit(solution)/shard_map/ppermute | solution.py:268
  121.0 2.2 %collective-permute-done.17 = f32[32,3]{1,0:T(8,128)S(1)} collective-permute-done((f32[32,3]{1,0:T(8,128)S(1)}, f32[32,3]{1,0:T(8,128)S(1)}, u32[]{:S(2)}, u32[]{:S(2)}) %collective-permute-start.17) | collective-permute-done | bytes 416 | tf_op jit(solution)/shard_map/ppermute | solution.py:268
  123.3 0.7 slice_reduce_fusion
  124.5 0.8 pad_maximum_fusion.1
  (33 shorter events, 3.1 us)
Async XLA Ops:
  11.4 3.1 %collective-permute-start = (f32[32,32,128]{2,1,0:T(8,128)}, f32[32,32,128]{2,1,0:T(8,128)S(1)}, u32[]{:S(2)}, u32[]{:S(2)}) collective-permute-start(f32[32,32,128]{2,1,0:T(8,128)} %get-tuple-element.32), channel_id=1, source_target_pairs={{0,4},{4,0},{8,12},{12,8},{16,20},{20,16},{24,28},{28,24},{1,5},{5... | collective-permute-start | bytes 1572872 | tf_op jit(solution)/shard_map/ppermute | solution.py:268
  12.0 7.3 %collective-permute-start.4 = (f32[32,32,128]{2,1,0:T(8,128)}, f32[32,32,128]{2,1,0:T(8,128)S(1)}, u32[]{:S(2)}, u32[]{:S(2)}) collective-permute-start(f32[32,32,128]{2,1,0:T(8,128)} %get-tuple-element.35), channel_id=1, source_target_pairs={{0,4},{4,0},{8,12},{12,8},{16,20},{20,16},{24,28},{28,24},{1,5},{5... | collective-permute-start | bytes 1572872 | tf_op jit(solution)/shard_map/ppermute | solution.py:268
  12.9 1.6 %collective-permute-start.1 = (f32[32]{0:T(128)S(1)}, f32[32]{0:T(128)S(1)}, u32[]{:S(2)}, u32[]{:S(2)}) collective-permute-start(f32[32]{0:T(128)S(1)} %slice_reduce_fusion.3), channel_id=1, source_target_pairs={{0,4},{4,0},{8,12},{12,8},{16,20},{20,16},{24,28},{28,24},{1,5},{5... | collective-permute-start | bytes 392 | tf_op jit(solution)/shard_map/ppermute | solution.py:268
  16.4 26.6 %collective-permute-start.2 = (f32[32,32,128]{2,1,0:T(8,128)}, f32[32,32,128]{2,1,0:T(8,128)S(1)}, u32[]{:S(2)}, u32[]{:S(2)}) collective-permute-start(f32[32,32,128]{2,1,0:T(8,128)} %select_add_fusion), channel_id=1, source_target_pairs={{0,8},{4,12},{8,0},{12,4},{16,24},{20,28},{24,16},{28,20},{1,9},{5... | collective-permute-start | bytes 1572872 | tf_op jit(solution)/shard_map/ppermute | solution.py:268
  19.3 38.6 %copy-start = (f32[32,32,128]{2,1,0:T(8,128)S(1)}, f32[32,32,128]{2,1,0:T(8,128)}, u32[]{:S(2)}) copy-start(f32[32,32,128]{2,1,0:T(8,128)} %get-tuple-element.33) | copy-start | bytes 1572868
  19.3 38.6 %copy-start.1 = (f32[32,32,128]{2,1,0:T(8,128)S(1)}, f32[32,32,128]{2,1,0:T(8,128)}, u32[]{:S(2)}) copy-start(f32[32,32,128]{2,1,0:T(8,128)} %get-tuple-element.36) | copy-start | bytes 1572868
  21.4 21.7 %collective-permute-start.5 = (f32[32,32,128]{2,1,0:T(8,128)}, f32[32,32,128]{2,1,0:T(8,128)S(1)}, u32[]{:S(2)}, u32[]{:S(2)}) collective-permute-start(f32[32,32,128]{2,1,0:T(8,128)} %multiply_add_fusion.2), channel_id=1, source_target_pairs={{0,8},{4,12},{8,0},{12,4},{16,24},{20,28},{24,16},{28,20},{1,9},{5... | collective-permute-start | bytes 1572872 | tf_op jit(solution)/shard_map/ppermute | solution.py:268
  21.4 21.7 %collective-permute-start.3 = (f32[32]{0:T(128)S(1)}, f32[32]{0:T(128)S(1)}, u32[]{:S(2)}, u32[]{:S(2)}) collective-permute-start(f32[32]{0:T(128)S(1)} %get-tuple-element.49), channel_id=1, source_target_pairs={{0,8},{4,12},{8,0},{12,4},{16,24},{20,28},{24,16},{28,20},{1,9},{5... | collective-permute-start | bytes 392 | tf_op jit(solution)/shard_map/ppermute | solution.py:268
  44.5 13.4 %collective-permute-start.6 = (f32[32,32,128]{2,1,0:T(8,128)S(1)}, f32[32,32,128]{2,1,0:T(8,128)S(1)}, u32[]{:S(2)}, u32[]{:S(2)}) collective-permute-start(f32[32,32,128]{2,1,0:T(8,128)S(1)} %select_select_fusion), channel_id=1, source_target_pairs={{0,16},{4,20},{8,24},{12,28},{16,0},{20,4},{24,8},{28,12},{1,17},{... | collective-permute-start | bytes 1572872 | tf_op jit(solution)/shard_map/ppermute | solution.py:268
  59.6 17.0 %collective-permute-start.7 = (f32[32,32,128]{2,1,0:T(8,128)}, f32[32,32,128]{2,1,0:T(8,128)S(1)}, u32[]{:S(2)}, u32[]{:S(2)}) collective-permute-start(f32[32,32,128]{2,1,0:T(8,128)} %get-tuple-element.66), channel_id=1, source_target_pairs={{0,4},{4,0},{8,12},{12,8},{16,20},{20,16},{24,28},{28,24},{1,5},{5... | collective-permute-start | bytes 1572872 | tf_op jit(solution)/shard_map/ppermute | solution.py:268
  59.6 17.0 %collective-permute-start.8 = (f32[32,32,128]{2,1,0:T(8,128)}, f32[32,32,128]{2,1,0:T(8,128)S(1)}, u32[]{:S(2)}, u32[]{:S(2)}) collective-permute-start(f32[32,32,128]{2,1,0:T(8,128)} %get-tuple-element.50), channel_id=1, source_target_pairs={{0,4},{4,0},{8,12},{12,8},{16,20},{20,16},{24,28},{28,24},{1,5},{5... | collective-permute-start | bytes 1572872 | tf_op jit(solution)/shard_map/ppermute | solution.py:268
  76.6 0.8 copy-start.2
  76.6 1.0 copy-start.3
  94.4 7.6 %collective-permute-start.11 = (f32[2,128,128]{2,1,0:T(8,128)S(1)}, f32[2,128,128]{2,1,0:T(8,128)S(1)}, u32[]{:S(2)}, u32[]{:S(2)}) collective-permute-start(f32[2,128,128]{2,1,0:T(8,128)S(1)} %get-tuple-element.63), channel_id=1, source_target_pairs={{0,3},{1,0},{2,1},{3,2},{4,7},{5,4},{6,5},{7,6},{8,11},{9,8},{10,9... | collective-permute-start | bytes 393224 | tf_op jit(solution)/shard_map/ppermute | solution.py:321
  98.0 11.5 %collective-permute-start.10 = (f32[2,128,128]{2,1,0:T(8,128)S(1)}, f32[2,128,128]{2,1,0:T(8,128)S(1)}, u32[]{:S(2)}, u32[]{:S(2)}) collective-permute-start(f32[2,128,128]{2,1,0:T(8,128)S(1)} %get-tuple-element.64), channel_id=1, source_target_pairs={{0,2},{1,3},{2,0},{3,1},{4,6},{5,7},{6,4},{7,5},{8,10},{9,11},{10,... | collective-permute-start | bytes 393224 | tf_op jit(solution)/shard_map/ppermute | solution.py:321
  98.0 11.5 %collective-permute-start.9 = (f32[2,128,128]{2,1,0:T(8,128)S(1)}, f32[2,128,128]{2,1,0:T(8,128)S(1)}, u32[]{:S(2)}, u32[]{:S(2)}) collective-permute-start(f32[2,128,128]{2,1,0:T(8,128)S(1)} %get-tuple-element.62), channel_id=1, source_target_pairs={{0,1},{1,2},{2,3},{3,0},{4,5},{5,6},{6,7},{7,4},{8,9},{9,10},{10,1... | collective-permute-start | bytes 393224 | tf_op jit(solution)/shard_map/ppermute | solution.py:321
  99.0 16.0 %collective-permute-start.15 = (f32[32,3]{1,0:T(8,128)}, f32[32,3]{1,0:T(8,128)S(1)}, u32[]{:S(2)}, u32[]{:S(2)}) collective-permute-start(f32[32,3]{1,0:T(8,128)} %bitcast.29), channel_id=1, source_target_pairs={{0,4},{4,0},{8,12},{12,8},{16,20},{20,16},{24,28},{28,24},{1,5},{5... | collective-permute-start | bytes 1160 | tf_op jit(solution)/shard_map/ppermute | solution.py:268
  110.4 13.6 %collective-permute-start.14 = (f32[2,128,128]{2,1,0:T(8,128)S(1)}, f32[2,128,128]{2,1,0:T(8,128)S(1)}, u32[]{:S(2)}, u32[]{:S(2)}) collective-permute-start(f32[2,128,128]{2,1,0:T(8,128)S(1)} %add_add_fusion), channel_id=1, source_target_pairs={{0,3},{1,0},{2,1},{3,2},{4,7},{5,4},{6,5},{7,6},{8,11},{9,8},{10,9... | collective-permute-start | bytes 393224 | tf_op jit(solution)/shard_map/ppermute | solution.py:321
  111.9 12.5 %collective-permute-start.13 = (f32[2,128,128]{2,1,0:T(8,128)S(1)}, f32[2,128,128]{2,1,0:T(8,128)S(1)}, u32[]{:S(2)}, u32[]{:S(2)}) collective-permute-start(f32[2,128,128]{2,1,0:T(8,128)S(1)} %add_add_fusion), channel_id=1, source_target_pairs={{0,2},{1,3},{2,0},{3,1},{4,6},{5,7},{6,4},{7,5},{8,10},{9,11},{10,... | collective-permute-start | bytes 393224 | tf_op jit(solution)/shard_map/ppermute | solution.py:321
  113.1 11.3 %collective-permute-start.12 = (f32[2,128,128]{2,1,0:T(8,128)S(1)}, f32[2,128,128]{2,1,0:T(8,128)S(1)}, u32[]{:S(2)}, u32[]{:S(2)}) collective-permute-start(f32[2,128,128]{2,1,0:T(8,128)S(1)} %add_add_fusion), channel_id=1, source_target_pairs={{0,1},{1,2},{2,3},{3,0},{4,5},{5,6},{6,7},{7,4},{8,9},{9,10},{10,1... | collective-permute-start | bytes 393224 | tf_op jit(solution)/shard_map/ppermute | solution.py:321
  115.8 3.7 %collective-permute-start.16 = (f32[32,3]{1,0:T(8,128)S(1)}, f32[32,3]{1,0:T(8,128)S(1)}, u32[]{:S(2)}, u32[]{:S(2)}) collective-permute-start(f32[32,3]{1,0:T(8,128)S(1)} %slice_add_fusion), channel_id=1, source_target_pairs={{0,8},{4,12},{8,0},{12,4},{16,24},{20,28},{24,16},{28,20},{1,9},{5... | collective-permute-start | bytes 1160 | tf_op jit(solution)/shard_map/ppermute | solution.py:268
  119.5 3.7 %collective-permute-start.17 = (f32[32,3]{1,0:T(8,128)S(1)}, f32[32,3]{1,0:T(8,128)S(1)}, u32[]{:S(2)}, u32[]{:S(2)}) collective-permute-start(f32[32,3]{1,0:T(8,128)S(1)} %add.157), channel_id=1, source_target_pairs={{0,16},{4,20},{8,24},{12,28},{16,0},{20,4},{24,8},{28,12},{1,17},{... | collective-permute-start | bytes 1160 | tf_op jit(solution)/shard_map/ppermute | solution.py:268

commit v3 on v2

--- a/solution.py
+++ b/solution.py
@@ -284,27 +284,22 @@
     s_all = scale(log_odd) * s_even + s_odd
     r_all = r_even + scale(log_even) * r_odd
     log_all = log_even + log_odd
+    chips, chip = peers // 2, place // 2
+
+    def onward(value, step):
+        return lax.ppermute(value, axis, [(i, (i + 2 * step) % peers) for i in range(peers)])
+
+    got, logs = {}, {}
+    for step in range(1, chips):
+        logs[step] = onward(log_all, step)
+        got[step] = onward(jnp.where(chip + step < chips, s_all, r_all), step)
     s_pre, r_pre = jnp.zeros_like(s_all), jnp.zeros_like(r_all)
     s_log, r_log = jnp.zeros_like(log_all), jnp.zeros_like(log_all)
-    distance = 2
-    while distance < peers:
-        upper = (place // distance) % 2 == 1
-        final = distance * 2 >= peers
-        log_new = hypercube_shift(log_all, axis, distance)
-        if final:
-            s_new = r_new = hypercube_shift(jnp.where(upper, r_all, s_all), axis, distance)
-        else:
-            s_new = hypercube_shift(s_all, axis, distance)
-            r_new = hypercube_shift(r_all, axis, distance)
-        s_pre = jnp.where(upper, s_pre + scale(s_log) * s_new, s_pre)
-        r_pre = jnp.where(upper, r_pre, r_pre + scale(r_log) * r_new)
-        if not final:
-            s_log = jnp.where(upper, s_log + log_new, s_log)
-            r_log = jnp.where(upper, r_log, r_log + log_new)
-            s_all = jnp.where(upper, scale(log_all) * s_new + s_all, scale(log_new) * s_all + s_new)
-            r_all = jnp.where(upper, r_new + scale(log_new) * r_all, r_all + scale(log_all) * r_new)
-            log_all = log_all + log_new
-        distance *= 2
+    for step in range(1, chips):
+        back = chips - step
+        s_pre = s_pre + jnp.where(chip >= step, scale(s_log), 0.0) * got[step]
+        r_pre = r_pre + jnp.where(chip + step < chips, scale(r_log), 0.0) * got[back]
+        s_log, r_log = s_log + logs[step], r_log + logs[back]
     s_for_odd = s_even + scale(log_even) * s_pre
     r_for_even = r_odd + scale(log_odd) * r_pre
     s_keep, s_give = jnp.where(odd, s_for_odd, s_pre), jnp.where(odd, s_pre, s_for_odd)

time: 126 us -> 118 us (0.937)
  waiting for transfers between devices: 47.6 us -> 40.2 us
    ppermute x12 -> x8, waiting for transfers between devices: 36.8 us -> 7.4 us  [hypercube_shift(): return lax.ppermute(value, axis, [(i, i ^ distance) for i in range(peers)])]
    ppermute x0 -> x6, waiting for transfers between devices: none -> 21.8 us  [onward(): lax.ppermute(value, axis, [(i, (i + 2 * step) % peers) for i in range(pee...]
    ppermute x0 -> x6, starting transfers between devices: none -> 9.46 us  [onward(): lax.ppermute(value, axis, [(i, (i + 2 * step) % peers) for i in range(pee...]
    ppermute x12 -> x8, starting transfers between devices: 11.4 us -> 2.89 us  [hypercube_shift(): return lax.ppermute(value, axis, [(i, i ^ distance) for i in range(peers)])]
    add x2 -> x1, other arithmetic: 4.05 us -> 0.01 us  [carried(): log_all = log_even + log_odd]
    select_n x1 -> x4, other arithmetic: 1.46 us -> 3.64 us  [the longest x2 2.42 us: carried(): got[step] = onward(jnp.where(chip + step < chips, s_all, r_all), step)]
  transfers between devices with their start and end apart: 18 -> 20, of which waited for: 8 -> 8; matrix products, arithmetic and copies ran while one was open for 6% -> 5% of each run, Pallas kernels for 13% -> 14%
where the time goes in v3:
time: 118 us
  Pallas kernels  41.6 us (35%)
  waiting for transfers between devices  40.2 us (34%)
  starting transfers between devices  21.6 us (18%)
  other arithmetic  9.24 us (8%)
  local copies, waits for them, and re-layouts  4.34 us (4%)
    ppermute x6, waiting for transfers between devices, onward(): lax.ppermute(value, axis, [(i, (i + 2 * step) % peers) for i in range(pee...  21.8 us
    pallas_call x1, Pallas kernels, on_device(): pl.pallas_call(within_kernel, grid=grid, in_specs=[tokens_by_wide, wide_b...  16.5 us
    pallas_call x1, Pallas kernels, on_device(): pl.pallas_call(across_kernel, grid=grid, in_specs=[scalar, tokens_by_wide...  15.7 us
    ppermute x6, waiting for transfers between devices, shift(): lax.ppermute(piece, axis, [(i, (i + step) % peers) for i in range(peers)])  10.9 us
    ppermute x6, starting transfers between devices, onward(): lax.ppermute(value, axis, [(i, (i + 2 * step) % peers) for i in range(pee...  9.46 us
    pallas_call x1, Pallas kernels, on_device(): pl.pallas_call(states_kernel, grid=grid, in_specs=[scalar, tokens_by_wide...  9.37 us
    ppermute x6, starting transfers between devices, shift(): lax.ppermute(piece, axis, [(i, (i + step) % peers) for i in range(peers)])  9.27 us
    ppermute x8, waiting for transfers between devices, hypercube_shift(): return lax.ppermute(value, axis, [(i, i ^ distance) for i in range(peers)])  7.4 us
  transfers between devices with their start and end apart: 20, of which 8 were waited for; matrix products, arithmetic and copies ran while one was open for 5% of the time, Pallas kernels for 14%

profile of v3, /device:TPU:0, one launch (start us, length us, event | category | flops | bytes accessed | tf_op | source)
XLA Modules:
  0.0 117.7 jit_solution(11623475003005738141)
XLA Ops:
  2.0 9.4 %states.1 = (bf16[2048,512]{1,0:T(8,128)(2,1)}, bf16[2048,512]{1,0:T(8,128)(2,1)}, f32[32,512]{1,0:T(8,128)}, f32[32,512]{1,0:T(8,128)}, f32[32,128]{1,0:T(8,128...) custom-call(s32[1]{0:T(128)} %bitcast.odd_ref, ...), custom_call_target="tpu_custom_call" | custom-call | tf_op jit(solution)/shard_map/states/pallas_call | solution.py:362
  12.0 0.8 slice_reduce_fusion.3
  13.4 1.1 collective-permute-done.1
  14.5 1.5 %broadcast_select_fusion.2 = (f32[32,32,128]{2,1,0:T(8,128)S(1)}, f32[32,32,128]{2,1,0:T(8,128)S(1)}, f32[32,32,128]{2,1,0:T(8,128)S(1)}) fusion(pred[]{:T(512)S(6)} %lt.73, f32[32,32,128]{2,1,0:T(8,128)} %get-tuple-element.36, f32[32,32,128]{2,1,0:T(8,128)S(1)} %collective-permute-done.2, f32[32]{0:T(128)S(1)} %get-tuple-element.72, pred[]{:T(512)S(6)} %eq.13, ...), kind=kLoop, calls=%fused_computation.15 | loop fusion | flops 1179648 | bytes 3670274 | tf_op jit(solution)/shard_map/jit(_where)/select_n | solution.py:295
  16.0 2.9 %collective-permute-start.3 = (f32[32,32,128]{2,1,0:T(8,128)S(1)}, f32[32,32,128]{2,1,0:T(8,128)}, u32[]{:S(2)}, u32[]{:S(2)}) collective-permute-start(f32[32,32,128]{2,1,0:T(8,128)S(1)} %get-tuple-element.52), channel_id=1, source_target_pairs={{0,8},{4,12},{8,16},{12,20},{16,24},{20,28},{24,0},{28,4},{1,9},{5... | collective-permute-start | bytes 1572872 | tf_op jit(solution)/shard_map/ppermute | solution.py:290
  18.9 0.9 broadcast_select_fusion.1
  19.8 1.5 %collective-permute-start.5 = (f32[32,32,128]{2,1,0:T(8,128)}, f32[32,32,128]{2,1,0:T(8,128)}, u32[]{:S(2)}, u32[]{:S(2)}) collective-permute-start(f32[32,32,128]{2,1,0:T(8,128)} %get-tuple-element.57), channel_id=1, source_target_pairs={{0,16},{4,20},{8,24},{12,28},{16,0},{20,4},{24,8},{28,12},{1,17},{... | collective-permute-start | bytes 1572872 | tf_op jit(solution)/shard_map/ppermute | solution.py:290
  21.3 1.4 %collective-permute-start.7 = (f32[32,32,128]{2,1,0:T(8,128)S(1)}, f32[32,32,128]{2,1,0:T(8,128)}, u32[]{:S(2)}, u32[]{:S(2)}) collective-permute-start(f32[32,32,128]{2,1,0:T(8,128)S(1)} %get-tuple-element.58), channel_id=1, source_target_pairs={{0,24},{4,28},{8,0},{12,4},{16,8},{20,12},{24,16},{28,20},{1,25},{... | collective-permute-start | bytes 1572872 | tf_op jit(solution)/shard_map/ppermute | solution.py:290
  23.3 1.5 %collective-permute-start.6 = (f32[32]{0:T(128)S(1)}, f32[32]{0:T(128)S(1)}, u32[]{:S(2)}, u32[]{:S(2)}) collective-permute-start(f32[32]{0:T(128)S(1)} %get-tuple-element.70), channel_id=1, source_target_pairs={{0,16},{4,20},{8,24},{12,28},{16,0},{20,4},{24,8},{28,12},{1,17},{... | collective-permute-start | bytes 392 | tf_op jit(solution)/shard_map/ppermute | solution.py:290
  24.8 18.9 %collective-permute-done.9 = f32[32]{0:T(128)S(1)} collective-permute-done((f32[32]{0:T(128)S(1)}, f32[32]{0:T(128)S(1)}, u32[]{:S(2)}, u32[]{:S(2)}) %collective-permute-start.9) | collective-permute-done | bytes 160 | tf_op jit(solution)/shard_map/ppermute | solution.py:290
  43.7 1.5 %collective-permute-start.4 = (f32[32]{0:T(128)S(1)}, f32[32]{0:T(128)S(1)}, u32[]{:S(2)}, u32[]{:S(2)}) collective-permute-start(f32[32]{0:T(128)S(1)} %get-tuple-element.70), channel_id=1, source_target_pairs={{0,8},{4,12},{8,16},{12,20},{16,24},{20,28},{24,0},{28,4},{1,9},{5... | collective-permute-start | bytes 392 | tf_op jit(solution)/shard_map/ppermute | solution.py:290
  45.3 2.9 %collective-permute-done.4 = f32[32]{0:T(128)S(1)} collective-permute-done((f32[32]{0:T(128)S(1)}, f32[32]{0:T(128)S(1)}, u32[]{:S(2)}, u32[]{:S(2)}) %collective-permute-start.4) | collective-permute-done | bytes 160 | tf_op jit(solution)/shard_map/ppermute | solution.py:290
  48.3 1.8 %fusion = (f32[32,32,128]{2,1,0:T(8,128)S(1)}, f32[32,32,128]{2,1,0:T(8,128)S(1)}, f32[32,32,128]{2,1,0:T(8,128)S(1)}, f32[32,32,128]{2,1,0:T(8,128)S(1)}) fusion(f32[32]{0:T(128)S(1)} %get-tuple-element.71, pred[]{:T(512)S(6)} %eq.13, f32[32,32,128]{2,1,0:T(8,128)S(1)} %copy-done.1, f32[32,32,128]{2,1,0:T(8,128)S(1)} %collective-permute-done.2, ...), kind=kLoop, calls=%fused_computation.2 | loop fusion | flops 2359296 | bytes 5767945 | tf_op jit(solution)/shard_map/jit(_where)/select_n | solution.py:306
  50.6 16.5 %within.1 = (f32[2048,512]{1,0:T(8,128)}, f32[32,512]{1,0:T(8,128)}, f32[32,512]{1,0:T(8,128)}, f32[4,128,128]{2,1,0:T(8,128)}) custom-call(bf16[512,2048]{1,0:T(8,128)(2,1)} %x_ref.5, bf16[2048,512]{1,0:T(8,128)(2,1)} %get-tuple-element.26.xt_ref, bf16[2048,512]{1,0:T(8,128)(2,1)} %get-tuple-element.27.gt_ref, f32[32,512]{1,0:T(8,128)} %get-tuple-element.28.dt_ref, ...), custom_call_target="tpu_custom_call" | custom-call | flops 3221225472 | bytes 14680064 | tf_op jit(solution)/shard_map/within/pallas_call | solution.py:378
  67.1 1.2 %fusion.1 = (f32[32,32,128]{2,1,0:T(8,128)}, f32[32,32,128]{2,1,0:T(8,128)}) fusion(f32[32,32,128]{2,1,0:T(8,128)S(1)} %get-tuple-element.49, f32[32]{0:T(128)S(1)} %get-tuple-element.71, pred[]{:T(512)S(6)} %eq.13, f32[32,32,128]{2,1,0:T(8,128)S(1)} %copy-done.1, f32[32,32,128]{2,1,0:T(8,128)S(1)} %collective-permute-done.2, ...), kind=kLoop, calls=%fused_computation.3 | loop fusion | flops 1048576 | bytes 4194561 | tf_op jit(solution)/shard_map/jit(_where)/select_n | solution.py:306
  68.3 0.8 copy-done.2
  69.3 15.7 %across.1 = (bf16[512,2048]{1,0:T(8,128)(2,1)}, f32[32,512]{1,0:T(8,128)}, f32[32,128]{1,0:T(8,128)}, f32[2,512,128]{2,1,0:T(8,128)}) custom-call(s32[1]{0:T(128)} %bitcast.odd_ref, bf16[512,2048]{1,0:T(8,128)(2,1)} %x_ref.5, bf16[512,2048]{1,0:T(8,128)(2,1)} %g_ref.3, bf16[2048,512]{1,0:T(8,128)(2,1)} %get-tuple-element.26.xt_ref, ...), custom_call_target="tpu_custom_call" | custom-call | tf_op jit(solution)/shard_map/across/pallas_call | solution.py:395
  85.0 1.1 constant_dynamic-slice_fusion.2
  86.1 3.6 %collective-permute-start.13 = (f32[2,128,128]{2,1,0:T(8,128)S(1)}, f32[2,128,128]{2,1,0:T(8,128)S(1)}, u32[]{:S(2)}, u32[]{:S(2)}) collective-permute-start(f32[2,128,128]{2,1,0:T(8,128)S(1)} %get-tuple-element.68), channel_id=1, source_target_pairs={{0,3},{1,0},{2,1},{3,2},{4,7},{5,4},{6,5},{7,6},{8,11},{9,8},{10,9... | collective-permute-start | bytes 393224 | tf_op jit(solution)/shard_map/ppermute | solution.py:316
  89.7 1.0 collective-permute-start.11
  90.8 2.9 %collective-permute-done.13 = f32[2,128,128]{2,1,0:T(8,128)S(1)} collective-permute-done((f32[2,128,128]{2,1,0:T(8,128)S(1)}, f32[2,128,128]{2,1,0:T(8,128)S(1)}, u32[]{:S(2)}, u32[]{:S(2)}) %collective-permute-start.13) | collective-permute-done | bytes 131104 | tf_op jit(solution)/shard_map/ppermute | solution.py:316
  93.7 7.6 %collective-permute-done.12 = f32[2,128,128]{2,1,0:T(8,128)S(1)} collective-permute-done((f32[2,128,128]{2,1,0:T(8,128)S(1)}, f32[2,128,128]{2,1,0:T(8,128)S(1)}, u32[]{:S(2)}, u32[]{:S(2)}) %collective-permute-start.12) | collective-permute-done | bytes 131104 | tf_op jit(solution)/shard_map/ppermute | solution.py:316
  101.3 0.9 add_add_fusion
  102.2 1.5 %collective-permute-start.16 = (f32[2,128,128]{2,1,0:T(8,128)S(1)}, f32[2,128,128]{2,1,0:T(8,128)S(1)}, u32[]{:S(2)}, u32[]{:S(2)}) collective-permute-start(f32[2,128,128]{2,1,0:T(8,128)S(1)} %add_add_fusion), channel_id=1, source_target_pairs={{0,3},{1,0},{2,1},{3,2},{4,7},{5,4},{6,5},{7,6},{8,11},{9,8},{10,9... | collective-permute-start | bytes 393224 | tf_op jit(solution)/shard_map/ppermute | solution.py:316
  103.8 1.1 collective-permute-start.15
  104.9 1.9 %collective-permute-start.14 = (f32[2,128,128]{2,1,0:T(8,128)S(1)}, f32[2,128,128]{2,1,0:T(8,128)S(1)}, u32[]{:S(2)}, u32[]{:S(2)}) collective-permute-start(f32[2,128,128]{2,1,0:T(8,128)S(1)} %add_add_fusion), channel_id=1, source_target_pairs={{0,1},{1,2},{2,3},{3,0},{4,5},{5,6},{6,7},{7,4},{8,9},{9,10},{10,1... | collective-permute-start | bytes 393224 | tf_op jit(solution)/shard_map/ppermute | solution.py:316
  106.9 0.7 slice_add_fusion
  108.2 3.1 %collective-permute-done.18 = f32[32,3]{1,0:T(8,128)S(1)} collective-permute-done((f32[32,3]{1,0:T(8,128)S(1)}, f32[32,3]{1,0:T(8,128)S(1)}, u32[]{:S(2)}, u32[]{:S(2)}) %collective-permute-start.18) | collective-permute-done | bytes 416 | tf_op jit(solution)/shard_map/ppermute | solution.py:268
  111.8 3.2 %collective-permute-done.19 = f32[32,3]{1,0:T(8,128)S(1)} collective-permute-done((f32[32,3]{1,0:T(8,128)S(1)}, f32[32,3]{1,0:T(8,128)S(1)}, u32[]{:S(2)}, u32[]{:S(2)}) %collective-permute-start.19) | collective-permute-done | bytes 416 | tf_op jit(solution)/shard_map/ppermute | solution.py:268
  115.1 0.7 slice_reduce_fusion
  116.3 0.7 pad_maximum_fusion.1
  117.0 0.7 pad_maximum_fusion.2
  (38 shorter events, 5.5 us)
Async XLA Ops:
  11.4 3.1 %collective-permute-start.2 = (f32[32,32,128]{2,1,0:T(8,128)}, f32[32,32,128]{2,1,0:T(8,128)S(1)}, u32[]{:S(2)}, u32[]{:S(2)}) collective-permute-start(f32[32,32,128]{2,1,0:T(8,128)} %get-tuple-element.35), channel_id=1, source_target_pairs={{0,4},{4,0},{8,12},{12,8},{16,20},{20,16},{24,28},{28,24},{1,5},{5... | collective-permute-start | bytes 1572872 | tf_op jit(solution)/shard_map/ppermute | solution.py:268
  12.0 2.5 %collective-permute-start = (f32[32,32,128]{2,1,0:T(8,128)}, f32[32,32,128]{2,1,0:T(8,128)S(1)}, u32[]{:S(2)}, u32[]{:S(2)}) collective-permute-start(f32[32,32,128]{2,1,0:T(8,128)} %get-tuple-element.32), channel_id=1, source_target_pairs={{0,4},{4,0},{8,12},{12,8},{16,20},{20,16},{24,28},{28,24},{1,5},{5... | collective-permute-start | bytes 1572872 | tf_op jit(solution)/shard_map/ppermute | solution.py:268
  12.9 1.6 %collective-permute-start.1 = (f32[32]{0:T(128)S(1)}, f32[32]{0:T(128)S(1)}, u32[]{:S(2)}, u32[]{:S(2)}) collective-permute-start(f32[32]{0:T(128)S(1)} %slice_reduce_fusion.3), channel_id=1, source_target_pairs={{0,4},{4,0},{8,12},{12,8},{16,20},{20,16},{24,28},{28,24},{1,5},{5... | collective-permute-start | bytes 392 | tf_op jit(solution)/shard_map/ppermute | solution.py:268
  14.5 33.8 %copy-start = (f32[32,32,128]{2,1,0:T(8,128)S(1)}, f32[32,32,128]{2,1,0:T(8,128)}, u32[]{:S(2)}) copy-start(f32[32,32,128]{2,1,0:T(8,128)} %get-tuple-element.33) | copy-start | bytes 1572868
  14.5 33.8 %copy-start.1 = (f32[32,32,128]{2,1,0:T(8,128)S(1)}, f32[32,32,128]{2,1,0:T(8,128)}, u32[]{:S(2)}) copy-start(f32[32,32,128]{2,1,0:T(8,128)} %get-tuple-element.36) | copy-start | bytes 1572868
  16.0 32.2 %collective-permute-start.3 = (f32[32,32,128]{2,1,0:T(8,128)S(1)}, f32[32,32,128]{2,1,0:T(8,128)}, u32[]{:S(2)}, u32[]{:S(2)}) collective-permute-start(f32[32,32,128]{2,1,0:T(8,128)S(1)} %get-tuple-element.52), channel_id=1, source_target_pairs={{0,8},{4,12},{8,16},{12,20},{16,24},{20,28},{24,0},{28,4},{1,9},{5... | collective-permute-start | bytes 1572872 | tf_op jit(solution)/shard_map/ppermute | solution.py:290
  19.8 28.4 %collective-permute-start.5 = (f32[32,32,128]{2,1,0:T(8,128)}, f32[32,32,128]{2,1,0:T(8,128)}, u32[]{:S(2)}, u32[]{:S(2)}) collective-permute-start(f32[32,32,128]{2,1,0:T(8,128)} %get-tuple-element.57), channel_id=1, source_target_pairs={{0,16},{4,20},{8,24},{12,28},{16,0},{20,4},{24,8},{28,12},{1,17},{... | collective-permute-start | bytes 1572872 | tf_op jit(solution)/shard_map/ppermute | solution.py:290
  21.3 26.9 %collective-permute-start.7 = (f32[32,32,128]{2,1,0:T(8,128)S(1)}, f32[32,32,128]{2,1,0:T(8,128)}, u32[]{:S(2)}, u32[]{:S(2)}) collective-permute-start(f32[32,32,128]{2,1,0:T(8,128)S(1)} %get-tuple-element.58), channel_id=1, source_target_pairs={{0,24},{4,28},{8,0},{12,4},{16,8},{20,12},{24,16},{28,20},{1,25},{... | collective-permute-start | bytes 1572872 | tf_op jit(solution)/shard_map/ppermute | solution.py:290
  22.8 21.0 %collective-permute-start.9 = (f32[32]{0:T(128)S(1)}, f32[32]{0:T(128)S(1)}, u32[]{:S(2)}, u32[]{:S(2)}) collective-permute-start(f32[32]{0:T(128)S(1)} %get-tuple-element.70), channel_id=1, source_target_pairs={{0,24},{4,28},{8,0},{12,4},{16,8},{20,12},{24,16},{28,20},{1,25},{... | collective-permute-start | bytes 392 | tf_op jit(solution)/shard_map/ppermute | solution.py:290
  23.3 22.0 %collective-permute-start.6 = (f32[32]{0:T(128)S(1)}, f32[32]{0:T(128)S(1)}, u32[]{:S(2)}, u32[]{:S(2)}) collective-permute-start(f32[32]{0:T(128)S(1)} %get-tuple-element.70), channel_id=1, source_target_pairs={{0,16},{4,20},{8,24},{12,28},{16,0},{20,4},{24,8},{28,12},{1,17},{... | collective-permute-start | bytes 392 | tf_op jit(solution)/shard_map/ppermute | solution.py:290
  43.7 4.5 %collective-permute-start.4 = (f32[32]{0:T(128)S(1)}, f32[32]{0:T(128)S(1)}, u32[]{:S(2)}, u32[]{:S(2)}) collective-permute-start(f32[32]{0:T(128)S(1)} %get-tuple-element.70), channel_id=1, source_target_pairs={{0,8},{4,12},{8,16},{12,20},{16,24},{20,28},{24,0},{28,4},{1,9},{5... | collective-permute-start | bytes 392 | tf_op jit(solution)/shard_map/ppermute | solution.py:290
  50.0 18.2 %collective-permute-start.8 = (f32[32,32,128]{2,1,0:T(8,128)S(1)}, f32[32,32,128]{2,1,0:T(8,128)S(1)}, u32[]{:S(2)}, u32[]{:S(2)}) collective-permute-start(f32[32,32,128]{2,1,0:T(8,128)S(1)} %get-tuple-element.55), channel_id=1, source_target_pairs={{0,4},{4,0},{8,12},{12,8},{16,20},{20,16},{24,28},{28,24},{1,5},{5... | collective-permute-start | bytes 1572872 | tf_op jit(solution)/shard_map/ppermute | solution.py:268
  50.1 18.2 %collective-permute-start.10 = (f32[32,32,128]{2,1,0:T(8,128)S(1)}, f32[32,32,128]{2,1,0:T(8,128)S(1)}, u32[]{:S(2)}, u32[]{:S(2)}) collective-permute-start(f32[32,32,128]{2,1,0:T(8,128)S(1)} %get-tuple-element.48), channel_id=1, source_target_pairs={{0,4},{4,0},{8,12},{12,8},{16,20},{20,16},{24,28},{28,24},{1,5},{5... | collective-permute-start | bytes 1572872 | tf_op jit(solution)/shard_map/ppermute | solution.py:268
  68.3 0.8 copy-start.2
  68.3 1.0 copy-start.3
  86.1 7.6 %collective-permute-start.13 = (f32[2,128,128]{2,1,0:T(8,128)S(1)}, f32[2,128,128]{2,1,0:T(8,128)S(1)}, u32[]{:S(2)}, u32[]{:S(2)}) collective-permute-start(f32[2,128,128]{2,1,0:T(8,128)S(1)} %get-tuple-element.68), channel_id=1, source_target_pairs={{0,3},{1,0},{2,1},{3,2},{4,7},{5,4},{6,5},{7,6},{8,11},{9,8},{10,9... | collective-permute-start | bytes 393224 | tf_op jit(solution)/shard_map/ppermute | solution.py:316
  89.7 11.6 %collective-permute-start.12 = (f32[2,128,128]{2,1,0:T(8,128)S(1)}, f32[2,128,128]{2,1,0:T(8,128)S(1)}, u32[]{:S(2)}, u32[]{:S(2)}) collective-permute-start(f32[2,128,128]{2,1,0:T(8,128)S(1)} %get-tuple-element.69), channel_id=1, source_target_pairs={{0,2},{1,3},{2,0},{3,1},{4,6},{5,7},{6,4},{7,5},{8,10},{9,11},{10,... | collective-permute-start | bytes 393224 | tf_op jit(solution)/shard_map/ppermute | solution.py:316
  89.7 11.6 %collective-permute-start.11 = (f32[2,128,128]{2,1,0:T(8,128)S(1)}, f32[2,128,128]{2,1,0:T(8,128)S(1)}, u32[]{:S(2)}, u32[]{:S(2)}) collective-permute-start(f32[2,128,128]{2,1,0:T(8,128)S(1)} %get-tuple-element.67), channel_id=1, source_target_pairs={{0,1},{1,2},{2,3},{3,0},{4,5},{5,6},{6,7},{7,4},{8,9},{9,10},{10,1... | collective-permute-start | bytes 393224 | tf_op jit(solution)/shard_map/ppermute | solution.py:316
  90.8 16.1 %collective-permute-start.17 = (f32[32,3]{1,0:T(8,128)}, f32[32,3]{1,0:T(8,128)S(1)}, u32[]{:S(2)}, u32[]{:S(2)}) collective-permute-start(f32[32,3]{1,0:T(8,128)} %bitcast.29), channel_id=1, source_target_pairs={{0,4},{4,0},{8,12},{12,8},{16,20},{20,16},{24,28},{28,24},{1,5},{5... | collective-permute-start | bytes 1160 | tf_op jit(solution)/shard_map/ppermute | solution.py:268
  102.2 13.6 %collective-permute-start.16 = (f32[2,128,128]{2,1,0:T(8,128)S(1)}, f32[2,128,128]{2,1,0:T(8,128)S(1)}, u32[]{:S(2)}, u32[]{:S(2)}) collective-permute-start(f32[2,128,128]{2,1,0:T(8,128)S(1)} %add_add_fusion), channel_id=1, source_target_pairs={{0,3},{1,0},{2,1},{3,2},{4,7},{5,4},{6,5},{7,6},{8,11},{9,8},{10,9... | collective-permute-start | bytes 393224 | tf_op jit(solution)/shard_map/ppermute | solution.py:316
  103.8 12.4 %collective-permute-start.15 = (f32[2,128,128]{2,1,0:T(8,128)S(1)}, f32[2,128,128]{2,1,0:T(8,128)S(1)}, u32[]{:S(2)}, u32[]{:S(2)}) collective-permute-start(f32[2,128,128]{2,1,0:T(8,128)S(1)} %add_add_fusion), channel_id=1, source_target_pairs={{0,2},{1,3},{2,0},{3,1},{4,6},{5,7},{6,4},{7,5},{8,10},{9,11},{10,... | collective-permute-start | bytes 393224 | tf_op jit(solution)/shard_map/ppermute | solution.py:316
  104.9 11.3 %collective-permute-start.14 = (f32[2,128,128]{2,1,0:T(8,128)S(1)}, f32[2,128,128]{2,1,0:T(8,128)S(1)}, u32[]{:S(2)}, u32[]{:S(2)}) collective-permute-start(f32[2,128,128]{2,1,0:T(8,128)S(1)} %add_add_fusion), channel_id=1, source_target_pairs={{0,1},{1,2},{2,3},{3,0},{4,5},{5,6},{6,7},{7,4},{8,9},{9,10},{10,1... | collective-permute-start | bytes 393224 | tf_op jit(solution)/shard_map/ppermute | solution.py:316
  107.6 3.7 %collective-permute-start.18 = (f32[32,3]{1,0:T(8,128)S(1)}, f32[32,3]{1,0:T(8,128)S(1)}, u32[]{:S(2)}, u32[]{:S(2)}) collective-permute-start(f32[32,3]{1,0:T(8,128)S(1)} %slice_add_fusion), channel_id=1, source_target_pairs={{0,8},{4,12},{8,0},{12,4},{16,24},{20,28},{24,16},{28,20},{1,9},{5... | collective-permute-start | bytes 1160 | tf_op jit(solution)/shard_map/ppermute | solution.py:268
  111.3 3.7 %collective-permute-start.19 = (f32[32,3]{1,0:T(8,128)S(1)}, f32[32,3]{1,0:T(8,128)S(1)}, u32[]{:S(2)}, u32[]{:S(2)}) collective-permute-start(f32[32,3]{1,0:T(8,128)S(1)} %add.163), channel_id=1, source_target_pairs={{0,16},{4,20},{8,24},{12,28},{16,0},{20,4},{24,8},{28,12},{1,17},{... | collective-permute-start | bytes 1160 | tf_op jit(solution)/shard_map/ppermute | solution.py:268
